TPU v7x, 128 devices: a whole 4x4x4 slice. The times are simulated.
128 devices in a mesh: ctx: 32 (over x, y, z_lo), tp: 4 (over z_hi, core).
Axes of the slice: x: 4, y: 4, z: 4 (z_hi: 2, z_lo: 2; z = z_hi * 2 + z_lo), core: 2. Of those that a mesh axis runs over, the one named last changes fastest.
Arguments:
- block_input: bfloat16 [4096, 1024], P(('ctx', 'tp')), may hold values from -6 to 6
- block_map: int32 [32], replicated, may hold values from 0 to 31, each once
- attn_gain: float32 [1024], replicated, may hold values from 0.1 to 1.9
- query_weight: bfloat16 [1024, 1024], P(None, 'tp'), may hold values from -0.1875 to 0.1875
- key_weight: bfloat16 [1024, 512], P(None, 'tp'), may hold values from -0.1875 to 0.1875
- value_weight: bfloat16 [1024, 512], P(None, 'tp'), may hold values from -0.1875 to 0.1875
- query_gain: float32 [64], replicated, may hold values from 0.5 to 2
- key_gain: float32 [64], replicated, may hold values from 0.5 to 2
- output_weight: bfloat16 [1024, 1024], P('tp'), may hold values from -3 to 3
- ffn_gain: float32 [1024], replicated, may hold values from 0.1 to 1.9
- gate_weight: bfloat16 [1024, 4608], P(None, 'tp'), may hold values from -0.1875 to 0.1875
- up_weight: bfloat16 [1024, 4608], P(None, 'tp'), may hold values from -0.1875 to 0.1875
- down_weight: bfloat16 [4608, 1024], P('tp'), may hold values from -0.09375 to 0.09375
- cotangent: bfloat16 [4096, 1024], P(('ctx', 'tp')), may hold values from -6 to 6
Outputs:
- block_output: float32 [4096, 1024], P(('ctx', 'tp'))
- input_grad: float32 [4096, 1024], P(('ctx', 'tp'))
- grad_attn_gain: float32 [1024], replicated
- grad_query: float32 [1024, 1024], P(None, 'tp')
- grad_key: float32 [1024, 512], P(None, 'tp')
- grad_value: float32 [1024, 512], P(None, 'tp')
- grad_query_gain: float32 [64], replicated
- grad_key_gain: float32 [64], replicated
- grad_output: float32 [1024, 1024], P('tp')
- grad_ffn_gain: float32 [1024], replicated
- grad_gate: float32 [1024, 4608], P(None, 'tp')
- grad_up: float32 [1024, 4608], P(None, 'tp')
- grad_down: float32 [4608, 1024], P('tp')
Inputs may be any that keep to these rules, and one draw needn't show every extreme that they name: Each value appears once; ctx index e holds, for sequence 0 and then sequence 1, the position blocks block_map[e] and 63 - block_map[e] of 32 tokens each, in that order.
All inputs are finite; a program needn't handle non-finite values.
Results may differ from a plain program's by a relative error of at most 0.034.
Values may be sent and summed in bfloat16 or wider, within the bound.
A program may use at most 128 MiB of HBM per device.

v0:
```python
import functools
import math

import jax
import jax.numpy as jnp
from jax import lax
from jax.experimental import pallas as pl
from jax.experimental.pallas import tpu as pltpu
from jax.sharding import PartitionSpec as P

MESH = pl.DeviceIdType.MESH
VMEM_LIMIT = 60 * 1024 * 1024


def _shifts(n):
    order = []
    for k in range(1, n // 2 + 1):
        order.append(k)
        if n - k != k:
            order.append(n - k)
    return order


def _enter(n, me, peer_axis):
    barrier = pltpu.get_barrier_semaphore()
    for k in _shifts(n):
        pl.semaphore_signal(
            barrier, 1, device_id=(lax.rem(me + k, n), peer_axis), device_id_type=MESH
        )
    pl.semaphore_wait(barrier, n - 1)


def _gather_kernel(n, part_ref, out_ref, send_sem, recv_sem):
    me = lax.axis_index("ctx")
    other = lax.axis_index("tp")
    rows = part_ref.shape[0]
    _enter(n, me, other)
    copies = []
    for k in _shifts(n):
        copy = pltpu.make_async_remote_copy(
            src_ref=part_ref,
            dst_ref=out_ref.at[pl.ds(pl.multiple_of(me * rows, rows), rows)],
            send_sem=send_sem.at[k],
            recv_sem=recv_sem.at[k],
            device_id=(lax.rem(me + k, n), other),
            device_id_type=MESH,
        )
        copy.start()
        copies.append(copy)
    out_ref[pl.ds(pl.multiple_of(me * rows, rows), rows), :] = part_ref[...]
    for k in _shifts(n):
        source = lax.rem(me + n - k, n)
        pltpu.make_async_remote_copy(
            src_ref=part_ref,
            dst_ref=out_ref.at[pl.ds(pl.multiple_of(source * rows, rows), rows)],
            send_sem=send_sem.at[k],
            recv_sem=recv_sem.at[k],
            device_id=(source, other),
            device_id_type=MESH,
        ).wait_recv()
    for copy in copies:
        copy.wait_send()


def ctx_gather(part, n, collective_id):
    rows, cols = part.shape
    return pl.pallas_call(
        functools.partial(_gather_kernel, n),
        out_shape=jax.ShapeDtypeStruct((n * rows, cols), part.dtype),
        in_specs=[pl.BlockSpec(memory_space=pltpu.VMEM)],
        out_specs=pl.BlockSpec(memory_space=pltpu.VMEM),
        scratch_shapes=[pltpu.SemaphoreType.DMA((n,)), pltpu.SemaphoreType.DMA((n,))],
        compiler_params=pltpu.CompilerParams(
            collective_id=collective_id, has_side_effects=True, vmem_limit_bytes=VMEM_LIMIT
        ),
    )(part)


def _scatter_sum(n, me, other, whole_ref, held, send_sem, recv_sem, rows):
    copies = []
    for k in _shifts(n):
        target = lax.rem(me + k, n)
        copy = pltpu.make_async_remote_copy(
            src_ref=whole_ref.at[pl.ds(pl.multiple_of(target * rows, rows), rows)],
            dst_ref=held.at[k],
            send_sem=send_sem.at[k],
            recv_sem=recv_sem.at[k],
            device_id=(target, other),
            device_id_type=MESH,
        )
        copy.start()
        copies.append(copy)
    total = whole_ref[pl.ds(pl.multiple_of(me * rows, rows), rows), :].astype(jnp.float32)
    for k in _shifts(n):
        source = lax.rem(me + n - k, n)
        pltpu.make_async_remote_copy(
            src_ref=whole_ref.at[pl.ds(0, rows)],
            dst_ref=held.at[k],
            send_sem=send_sem.at[k],
            recv_sem=recv_sem.at[k],
            device_id=(source, other),
            device_id_type=MESH,
        ).wait_recv()
        total = total + held[k].astype(jnp.float32)
    for copy in copies:
        copy.wait_send()
    return total


def _scatter_kernel(n, whole_ref, out_ref, held, send_sem, recv_sem):
    me = lax.axis_index("ctx")
    other = lax.axis_index("tp")
    rows = out_ref.shape[0]
    _enter(n, me, other)
    out_ref[...] = _scatter_sum(n, me, other, whole_ref, held, send_sem, recv_sem, rows)


def ctx_scatter(whole, n, collective_id):
    rows, cols = whole.shape[0] // n, whole.shape[1]
    return pl.pallas_call(
        functools.partial(_scatter_kernel, n),
        out_shape=jax.ShapeDtypeStruct((rows, cols), jnp.float32),
        in_specs=[pl.BlockSpec(memory_space=pltpu.VMEM)],
        out_specs=pl.BlockSpec(memory_space=pltpu.VMEM),
        scratch_shapes=[
            pltpu.VMEM((n, rows, cols), whole.dtype),
            pltpu.SemaphoreType.DMA((n,)),
            pltpu.SemaphoreType.DMA((n,)),
        ],
        compiler_params=pltpu.CompilerParams(
            collective_id=collective_id, has_side_effects=True, vmem_limit_bytes=VMEM_LIMIT
        ),
    )(whole)


def _shift_at(n, step):
    half = step // 2 + 1
    return jnp.where(step % 2 == 0, half, n - half)


def _sum_kernel(n, spans, whole_ref, extra_ref, out_ref, extra_out, *scratch):
    pieces = len(spans)
    helds, mines, extra_held = scratch[:pieces], scratch[pieces : 2 * pieces], scratch[2 * pieces]
    sems = scratch[2 * pieces + 1 :]
    send_extra, recv_extra = sems[4 * pieces], sems[4 * pieces + 1]
    me = lax.axis_index("ctx")
    other = lax.axis_index("tp")
    rows = whole_ref.shape[0] // n
    own_rows = pl.ds(pl.multiple_of(me * rows, rows), rows)
    _enter(n, me, other)

    def extra_copy(k, peer):
        return pltpu.make_async_remote_copy(
            src_ref=extra_ref,
            dst_ref=extra_held.at[k],
            send_sem=send_extra.at[k],
            recv_sem=recv_extra.at[k],
            device_id=(peer, other),
            device_id_type=MESH,
        )

    def scatter_copy(piece, k, peer, block):
        first, width = spans[piece]
        return pltpu.make_async_remote_copy(
            src_ref=whole_ref.at[pl.ds(pl.multiple_of(block * rows, rows), rows), pl.ds(first, width)],
            dst_ref=helds[piece].at[k],
            send_sem=sems[4 * piece].at[k],
            recv_sem=sems[4 * piece + 1].at[k],
            device_id=(peer, other),
            device_id_type=MESH,
        )

    def gather_copy(piece, k, peer, block):
        first, width = spans[piece]
        return pltpu.make_async_remote_copy(
            src_ref=mines[piece],
            dst_ref=out_ref.at[pl.ds(pl.multiple_of(block * rows, rows), rows), pl.ds(first, width)],
            send_sem=sems[4 * piece + 2].at[k],
            recv_sem=sems[4 * piece + 3].at[k],
            device_id=(peer, other),
            device_id_type=MESH,
        )

    def each_peer(body):
        def step(index, carry):
            k = _shift_at(n, index)
            return body(k, lax.rem(me + k, n), lax.rem(me + n - k, n), carry)

        return lax.fori_loop(0, n - 1, step, 0)

    def start_extra(k, target, source, carry):
        extra_copy(k, target).start()
        return carry

    each_peer(start_extra)
    for piece in range(pieces):

        def start_scatter(k, target, source, carry, piece=piece):
            scatter_copy(piece, k, target, target).start()
            return carry

        each_peer(start_scatter)
    for piece, (first, width) in enumerate(spans):

        def add_block(index, total, piece=piece):
            k = _shift_at(n, index)
            scatter_copy(piece, k, lax.rem(me + n - k, n), me).wait_recv()
            return total + helds[piece][k].astype(jnp.float32)

        total = lax.fori_loop(
            0, n - 1, add_block, whole_ref[own_rows, pl.ds(first, width)].astype(jnp.float32)
        )
        mines[piece][...] = total.astype(mines[piece].dtype)

        def start_gather(k, target, source, carry, piece=piece):
            gather_copy(piece, k, target, me).start()
            return carry

        each_peer(start_gather)
        out_ref[own_rows, pl.ds(first, width)] = mines[piece][...]

    def add_extra(index, total):
        k = _shift_at(n, index)
        extra_copy(k, lax.rem(me + n - k, n)).wait_recv()
        return total + extra_held[k]

    extra_out[...] = lax.fori_loop(0, n - 1, add_extra, extra_ref[...])
    for piece in range(pieces):

        def finish(k, target, source, carry, piece=piece):
            gather_copy(piece, k, source, source).wait_recv()
            gather_copy(piece, k, target, me).wait_send()
            scatter_copy(piece, k, target, target).wait_send()
            return carry

        each_peer(finish)

    def finish_extra(k, target, source, carry):
        extra_copy(k, target).wait_send()
        return carry

    each_peer(finish_extra)


def ctx_sum(whole, extra, n, collective_id, pieces=8):
    rows, cols = whole.shape[0] // n, whole.shape[1]
    lanes = cols // 128
    edges = [128 * (lanes * p // pieces) for p in range(pieces + 1)]
    spans = tuple((edges[p], edges[p + 1] - edges[p]) for p in range(pieces))
    return pl.pallas_call(
        functools.partial(_sum_kernel, n, spans),
        out_shape=(
            jax.ShapeDtypeStruct(whole.shape, whole.dtype),
            jax.ShapeDtypeStruct(extra.shape, extra.dtype),
        ),
        in_specs=[pl.BlockSpec(memory_space=pltpu.VMEM)] * 2,
        out_specs=(pl.BlockSpec(memory_space=pltpu.VMEM),) * 2,
        scratch_shapes=[pltpu.VMEM((n, rows, width), whole.dtype) for _, width in spans]
        + [pltpu.VMEM((rows, width), whole.dtype) for _, width in spans]
        + [pltpu.VMEM((n,) + extra.shape, extra.dtype)]
        + [pltpu.SemaphoreType.DMA((n,))] * (4 * pieces + 2),
        compiler_params=pltpu.CompilerParams(
            collective_id=collective_id, has_side_effects=True, vmem_limit_bytes=VMEM_LIMIT
        ),
    )(whole, extra)


EPS = 1e-05
THETA = 1000000.0
NEGATIVE = -1e30


def rms_forward(values, norm_gain):
    inverse = lax.rsqrt(jnp.mean(values * values, axis=-1, keepdims=True) + EPS)
    return (values * inverse * norm_gain, inverse)


def rms_backward(values, inverse, norm_gain, upstream):
    scaled = upstream * norm_gain
    inner_mean = jnp.mean(scaled * values, axis=-1, keepdims=True)
    through = inverse * (scaled - values * inverse * inverse * inner_mean)
    return (through, upstream * values * inverse)


def rope_tables(positions, head_dim):
    halfway = head_dim // 2
    frequency = THETA ** (-(jnp.arange(halfway, dtype=jnp.float32) * 2.0 / head_dim))
    angles = positions.astype(jnp.float32)[:, None] * frequency[None, :]
    return (jnp.cos(angles)[:, None, :], jnp.sin(angles)[:, None, :])


def rope_apply(values, cosine, sine_table):
    halfway = values.shape[-1] // 2
    first_half = values[..., :halfway]
    second_half = values[..., halfway:]
    return jnp.concatenate(
        [
            first_half * cosine - second_half * sine_table,
            second_half * cosine + first_half * sine_table,
        ],
        axis=-1,
    )


def rope_back(upstream, cosine, sine_table):
    halfway = upstream.shape[-1] // 2
    first_half = upstream[..., :halfway]
    second_half = upstream[..., halfway:]
    return jnp.concatenate(
        [
            first_half * cosine + second_half * sine_table,
            second_half * cosine - first_half * sine_table,
        ],
        axis=-1,
    )


def row_places(block_map, holder, rows_total, place_count):
    piece_len = rows_total // 4
    within = jnp.arange(rows_total, dtype=jnp.int32)
    picked = jnp.sum(jnp.where(jnp.arange(place_count, dtype=jnp.int32) == holder, block_map, 0))
    later = within // piece_len % 2
    piece_index = jnp.where(later == 1, 2 * place_count - 1 - picked, picked)
    return piece_index * piece_len + within % piece_len


def span_places(block_map, first_anchor, shard_span, seq_rows, place_count):
    piece_len = seq_rows // 2
    anchors = first_anchor + jnp.arange(shard_span, dtype=jnp.int32)
    picked = jnp.sum(
        jnp.where(
            jnp.arange(place_count, dtype=jnp.int32)[None, :] == anchors[:, None],
            block_map[None, :],
            0,
        ),
        axis=1,
    )
    within = jnp.arange(seq_rows, dtype=jnp.int32)
    later = within // piece_len % 2
    piece_index = jnp.where(
        later[None, :] == 1, 2 * place_count - 1 - picked[:, None], picked[:, None]
    )
    return (piece_index * piece_len + (within % piece_len)[None, :]).reshape(shard_span * seq_rows)


def gather_rows(rows_low):
    return lax.all_gather(rows_low, "tp", axis=0, tiled=True)


def reduce_rows(partial_rows):
    return lax.psum_scatter(
        partial_rows.astype(jnp.bfloat16), "tp", scatter_dimension=0, tiled=True
    ).astype(jnp.float32)


def per_device(
    block_input,
    block_map,
    attn_gain,
    query_weight,
    key_weight,
    value_weight,
    query_gain,
    key_gain,
    output_weight,
    ffn_gain,
    gate_weight,
    up_weight,
    down_weight,
    cotangent,
):
    place_count = lax.axis_size("ctx")
    place_index = lax.axis_index("ctx")
    head_dim = query_gain.shape[0]
    query_heads = query_weight.shape[1] // head_dim
    kv_heads = key_weight.shape[1] // head_dim
    group_size = query_heads // kv_heads
    score_scale = 1.0 / math.sqrt(head_dim)
    shard_span = 4
    residual_in = block_input.astype(jnp.float32)
    normed_one, inverse_one = rms_forward(residual_in, attn_gain)
    rows_one = gather_rows(normed_one.astype(jnp.bfloat16))
    rows_total = rows_one.shape[0]
    seq_rows = rows_total // 2
    kv_width = kv_heads * head_dim
    own_places = row_places(block_map, place_index, rows_total, place_count)
    query_raw = jnp.dot(rows_one, query_weight, preferred_element_type=jnp.float32).reshape(
        rows_total, query_heads, head_dim
    )
    key_raw = jnp.dot(rows_one, key_weight, preferred_element_type=jnp.float32).reshape(
        rows_total, kv_heads, head_dim
    )
    values_own = jnp.dot(rows_one, value_weight, preferred_element_type=jnp.float32).astype(
        jnp.bfloat16
    )
    query_normed, query_inverse = rms_forward(query_raw, query_gain)
    key_normed, key_inverse = rms_forward(key_raw, key_gain)
    cosine, sine_table = rope_tables(own_places, head_dim)
    query_rot = rope_apply(query_normed, cosine, sine_table).astype(jnp.bfloat16)
    keys_own = (
        rope_apply(key_normed, cosine, sine_table)
        .astype(jnp.bfloat16)
        .reshape(rows_total, kv_width)
    )
    query_blocks = query_rot.reshape(2, seq_rows, kv_heads, group_size, head_dim)
    query_places = own_places[:seq_rows]

    whole_kv = ctx_gather(jnp.concatenate([keys_own, values_own], axis=1), place_count, 0)
    seq_kv = jnp.transpose(
        whole_kv.reshape(place_count, 2, seq_rows, 2 * kv_width), (1, 0, 2, 3)
    ).reshape(2, place_count * seq_rows, 2 * kv_width)
    key_heads = seq_kv[..., :kv_width].reshape(2, place_count * seq_rows, kv_heads, head_dim)
    value_heads = seq_kv[..., kv_width:].reshape(2, place_count * seq_rows, kv_heads, head_dim)
    key_places = span_places(block_map, 0, place_count, seq_rows, place_count)
    allowed = key_places[None, :] <= query_places[:, None]
    scores = (
        jnp.einsum(
            "sqhgd,skhd->shgqk", query_blocks, key_heads, preferred_element_type=jnp.float32
        )
        * score_scale
    )
    top = jnp.max(jnp.where(allowed, scores, NEGATIVE), axis=-1)
    weights = jnp.where(allowed, jnp.exp(scores - top[..., None]), 0.0)
    weight_total = jnp.sum(weights, axis=-1)
    weighted = jnp.einsum(
        "shgqk,skhd->shgqd",
        weights.astype(jnp.bfloat16),
        value_heads,
        preferred_element_type=jnp.float32,
    )
    log_total = top + jnp.log(weight_total)
    attn_rows = jnp.transpose(weighted / weight_total[..., None], (0, 3, 1, 2, 4))
    attn_low = attn_rows.reshape(rows_total, query_heads * head_dim).astype(jnp.bfloat16)
    residual_mid = residual_in + reduce_rows(
        jnp.dot(attn_low, output_weight, preferred_element_type=jnp.float32)
    )
    normed_two, inverse_two = rms_forward(residual_mid, ffn_gain)
    rows_two = gather_rows(normed_two.astype(jnp.bfloat16))
    gate_pre = jnp.dot(rows_two, gate_weight, preferred_element_type=jnp.float32)
    up_pre = jnp.dot(rows_two, up_weight, preferred_element_type=jnp.float32)
    gate_sig = jax.nn.sigmoid(gate_pre)
    activated = (gate_pre * gate_sig * up_pre).astype(jnp.bfloat16)
    block_output = residual_mid + reduce_rows(
        jnp.dot(activated, down_weight, preferred_element_type=jnp.float32)
    )
    grad_rows = gather_rows(cotangent)
    grad_down_t = jnp.dot(grad_rows.T, activated, preferred_element_type=jnp.float32)
    grad_act = jnp.dot(grad_rows, down_weight.T, preferred_element_type=jnp.float32)
    grad_gate_pre = (grad_act * up_pre * gate_sig * (1.0 + gate_pre * (1.0 - gate_sig))).astype(
        jnp.bfloat16
    )
    grad_up_pre = (grad_act * gate_pre * gate_sig).astype(jnp.bfloat16)
    grad_gate = jnp.dot(rows_two.T, grad_gate_pre, preferred_element_type=jnp.float32)
    grad_up = jnp.dot(rows_two.T, grad_up_pre, preferred_element_type=jnp.float32)
    grad_normed_two = reduce_rows(
        jnp.dot(grad_gate_pre, gate_weight.T, preferred_element_type=jnp.float32)
        + jnp.dot(grad_up_pre, up_weight.T, preferred_element_type=jnp.float32)
    )
    through_two, ffn_terms = rms_backward(residual_mid, inverse_two, ffn_gain, grad_normed_two)
    grad_mid = cotangent.astype(jnp.float32) + through_two
    grad_mid_rows = gather_rows(grad_mid.astype(jnp.bfloat16))
    grad_output_t = jnp.dot(grad_mid_rows.T, attn_low, preferred_element_type=jnp.float32)
    grad_attn = jnp.dot(grad_mid_rows, output_weight.T, preferred_element_type=jnp.float32).astype(
        jnp.bfloat16
    )
    grad_attn_blocks = grad_attn.reshape(2, seq_rows, kv_heads, group_size, head_dim)
    delta_rows = jnp.sum(grad_attn_blocks.astype(jnp.float32) * attn_rows, axis=-1)
    delta_rows = jnp.transpose(delta_rows, (0, 2, 3, 1))

    probs = jnp.where(allowed, jnp.exp(scores - log_total[..., None]), 0.0)
    grad_value_seq = jnp.einsum(
        "shgqk,sqhgd->skhd",
        probs.astype(jnp.bfloat16),
        grad_attn_blocks,
        preferred_element_type=jnp.float32,
    )
    grad_probs = jnp.einsum(
        "sqhgd,skhd->shgqk", grad_attn_blocks, value_heads, preferred_element_type=jnp.float32
    )
    grad_scores = (score_scale * probs * (grad_probs - delta_rows[..., None])).astype(jnp.bfloat16)
    query_acc = jnp.einsum(
        "shgqk,skhd->sqhgd", grad_scores, key_heads, preferred_element_type=jnp.float32
    )
    grad_key_seq = jnp.einsum(
        "shgqk,sqhgd->skhd", grad_scores, query_blocks, preferred_element_type=jnp.float32
    )
    grad_kv_seq = jnp.concatenate(
        [
            grad_key_seq.reshape(2, place_count, seq_rows, kv_width),
            grad_value_seq.reshape(2, place_count, seq_rows, kv_width),
        ],
        axis=-1,
    )
    grad_kv_all = jnp.transpose(grad_kv_seq, (1, 0, 2, 3)).reshape(
        place_count * rows_total, 2 * kv_width
    )
    grad_kv_flat = ctx_scatter(
        grad_kv_all.astype(jnp.bfloat16),
        place_count,
        1,
    )
    grad_keys_flat, grad_values_flat = grad_kv_flat[:, :kv_width], grad_kv_flat[:, kv_width:]
    grad_query_rot = query_acc.reshape(rows_total, query_heads, head_dim)
    grad_key_rot = grad_keys_flat.reshape(rows_total, kv_heads, head_dim)
    grad_query_raw, query_terms = rms_backward(
        query_raw, query_inverse, query_gain, rope_back(grad_query_rot, cosine, sine_table)
    )
    grad_key_raw, key_terms = rms_backward(
        key_raw, key_inverse, key_gain, rope_back(grad_key_rot, cosine, sine_table)
    )
    grad_query_low = grad_query_raw.reshape(rows_total, query_heads * head_dim).astype(jnp.bfloat16)
    grad_key_low = grad_key_raw.reshape(rows_total, kv_width).astype(jnp.bfloat16)
    grad_value_low = grad_values_flat.astype(jnp.bfloat16)
    grad_query = jnp.dot(rows_one.T, grad_query_low, preferred_element_type=jnp.float32)
    grad_key = jnp.dot(rows_one.T, grad_key_low, preferred_element_type=jnp.float32)
    grad_value = jnp.dot(rows_one.T, grad_value_low, preferred_element_type=jnp.float32)
    grad_normed_one = reduce_rows(
        jnp.dot(grad_query_low, query_weight.T, preferred_element_type=jnp.float32)
        + jnp.dot(grad_key_low, key_weight.T, preferred_element_type=jnp.float32)
        + jnp.dot(grad_value_low, value_weight.T, preferred_element_type=jnp.float32)
    )
    through_one, attn_terms = rms_backward(residual_in, inverse_one, attn_gain, grad_normed_one)
    input_grad = grad_mid + through_one
    weight_parts = (grad_query, grad_key, grad_value, grad_output_t, grad_gate, grad_up, grad_down_t)
    widths = [part.shape[1] for part in weight_parts]
    gain_parts = (
        jnp.sum(attn_terms, axis=0),
        jnp.sum(query_terms, axis=(0, 1)),
        jnp.sum(key_terms, axis=(0, 1)),
        jnp.sum(ffn_terms, axis=0),
    )
    gain_sizes = [part.shape[0] for part in gain_parts]
    gain_flat = lax.psum(jnp.concatenate(gain_parts), "tp")
    gain_pad = -gain_flat.shape[0] % 1024
    summed, gains = ctx_sum(
        jnp.concatenate([part.astype(jnp.bfloat16) for part in weight_parts], axis=1),
        jnp.pad(gain_flat, (0, gain_pad)).reshape(8, -1),
        place_count,
        2,
    )
    summed = summed.astype(jnp.float32)
    gains = gains.reshape(-1)
    offsets = [sum(widths[:k]) for k in range(len(widths) + 1)]
    shared_query, shared_key, shared_value, output_t, shared_gate, shared_up, down_t = (
        summed[:, offsets[k] : offsets[k + 1]] for k in range(len(widths))
    )
    shared_output = output_t.T
    shared_down = down_t.T
    gain_attn = gains[: gain_sizes[0]]
    gain_query = gains[gain_sizes[0] : gain_sizes[0] + gain_sizes[1]]
    gain_key = gains[gain_sizes[0] + gain_sizes[1] : gain_sizes[0] + gain_sizes[1] + gain_sizes[2]]
    gain_ffn = gains[gain_sizes[0] + gain_sizes[1] + gain_sizes[2] : sum(gain_sizes)]
    return (
        block_output,
        input_grad,
        gain_attn,
        shared_query,
        shared_key,
        shared_value,
        gain_query,
        gain_key,
        shared_output,
        gain_ffn,
        shared_gate,
        shared_up,
        shared_down,
    )


def solution(mesh):
    return jax.shard_map(
        per_device,
        mesh=mesh,
        in_specs=(
            P(("ctx", "tp"), None),
            P(),
            P(),
            P(None, "tp"),
            P(None, "tp"),
            P(None, "tp"),
            P(),
            P(),
            P("tp", None),
            P(),
            P(None, "tp"),
            P(None, "tp"),
            P("tp", None),
            P(("ctx", "tp"), None),
        ),
        out_specs=(
            P(("ctx", "tp"), None),
            P(("ctx", "tp"), None),
            P(),
            P(None, "tp"),
            P(None, "tp"),
            P(None, "tp"),
            P(),
            P(),
            P("tp", None),
            P(),
            P(None, "tp"),
            P(None, "tp"),
            P("tp", None),
        ),
        check_vma=False,
    )
```

profile of v0, /device:TPU:28, one launch (start us, length us, event | category | flops | bytes accessed | tf_op | source)
XLA Modules:
  0.0 585.5 jit_solution(10642702818630612192)
XLA Ops:
  10.2 8.1 %all_gather.12 = bf16[128,1024]{1,0:T(8,128)(2,1)S(1)} all-gather(bf16[32,1024]{1,0:T(8,128)(2,1)S(1)} %fusion.43), channel_id=1, replica_groups=mesh['ctx'=32,'tp'=4] {'tp'}, dimensions={0}, use_global_device_ids=true | all-gather | bytes 327680 | tf_op jit(solution)/shard_map/all_gather | solution.py:347
  27.0 42.1 %shard_map.237 = bf16[4096,256]{1,0:T(8,128)(2,1)} custom-call(bf16[128,256]{1,0:T(8,128)(2,1)} %pad_maximum_fusion.2.part_ref), custom_call_target="tpu_custom_call" | custom-call | tf_op jit(solution)/shard_map/pallas_call | solution.py:67
  69.1 1.7 copy.76
  70.8 1.7 fusion.82
  72.5 1.5 copy.77
  74.0 2.0 fusion.86
  77.8 1.4 subtract_convert_fusion
  79.2 1.5 concatenate.38
  80.7 1.6 copy.79
  82.3 1.5 concatenate.39
  83.8 1.6 copy.80
  86.0 1.4 multiply_add_fusion.2
  87.4 1.4 add.168
  88.8 2.3 copy.81
  91.9 2.0 fusion.2
  95.2 2.0 fusion.85
  97.2 1.7 copy.82
  98.9 1.7 convert_element_type.134
  100.5 2.0 convolution_convert_fusion.8
  102.6 8.0 %all_gather.14 = bf16[128,1024]{1,0:T(8,128)(2,1)} all-gather(bf16[32,1024]{1,0:T(8,128)(2,1)S(1)} %copy-done.33), channel_id=1, replica_groups=mesh['ctx'=32,'tp'=4] {'tp'}, dimensions={0}, use_global_device_ids=true | all-gather | bytes 327680 | tf_op jit(solution)/shard_map/all_gather | solution.py:347
  110.6 20.3 %reduce-scatter.5.cloned.1.call-done = bf16[32,1024]{1,0:T(8,128)(2,1)} async-done(((bf16[128,1024]{1,0:T(8,128)(2,1)}), bf16[32,1024]{1,0:T(8,128)(2,1)}) %reduce-scatter.5.cloned.1.call-update) | async-done | bytes 65552 | tf_op jit(solution)/shard_map/reduce_scatter | solution.py:351
  133.0 7.3 %all_gather.13 = bf16[128,1024]{1,0:T(8,128)(2,1)S(1)} all-gather(bf16[32,1024]{1,0:T(8,128)(2,1)S(1)} %multiply_convert_fusion.3), channel_id=1, replica_groups=mesh['ctx'=32,'tp'=4] {'tp'}, dimensions={0}, use_global_device_ids=true | all-gather | bytes 327680 | tf_op jit(solution)/shard_map/all_gather | solution.py:347
  140.3 2.3 fusion.87
  143.2 1.7 multiply_convert_fusion
  145.8 1.6 fusion.31
  151.3 1.6 copy.90
  156.8 17.1 %reduce-scatter.9.cloned.1.call-done = bf16[32,1024]{1,0:T(8,128)(2,1)} async-done(((bf16[128,1024]{1,0:T(8,128)(2,1)}), bf16[32,1024]{1,0:T(8,128)(2,1)}) %reduce-scatter.9.cloned.1.call-update) | async-done | bytes 65552 | tf_op jit(solution)/shard_map/reduce_scatter | solution.py:351
  173.9 1.5 fusion.51
  177.0 7.5 %all_gather.15 = bf16[128,1024]{1,0:T(8,128)(2,1)S(1)} all-gather(bf16[32,1024]{1,0:T(8,128)(2,1)S(1)} %fusion.77), channel_id=1, replica_groups=mesh['ctx'=32,'tp'=4] {'tp'}, dimensions={0}, use_global_device_ids=true | all-gather | bytes 327680 | tf_op jit(solution)/shard_map/all_gather | solution.py:347
  185.2 2.0 convolution_convert_fusion.9
  187.2 1.6 reshape.328
  188.8 1.7 copy.84
  191.7 4.9 fusion.16
  196.7 1.7 fusion.1
  198.4 1.5 fusion.17
  200.0 1.8 convolution_bitcast_fusion.2
  201.8 4.4 reshape.330
  206.2 4.4 reshape.331
  210.6 5.0 maximum_bitcast_fusion
  215.6 5.5 copy.93
  221.2 42.9 %shard_map.238 = f32[128,256]{1,0:T(8,128)} custom-call(bf16[4096,256]{1,0:T(8,128)(2,1)} %bitcast.191), custom_call_target="tpu_custom_call" | custom-call | tf_op jit(solution)/shard_map/pallas_call | solution.py:120
  266.3 1.9 copy.85
  270.7 1.7 copy.89
  272.3 1.7 copy.86
  278.0 1.9 fusion.28
  280.2 2.2 convolution_convert_fusion.7
  282.4 2.1 fusion.27
  284.7 1.8 fusion.30
  286.5 1.9 fusion.29
  288.4 2.0 fusion.26
  290.4 3.3 fusion.8
  293.7 2.3 fusion.7
  296.0 2.4 fusion.10.whole_ref
  298.3 8.0 %reduce-scatter.11.cloned.1.call-done = bf16[32,1024]{1,0:T(8,128)(2,1)} async-done(((bf16[128,1024]{1,0:T(8,128)(2,1)}), bf16[32,1024]{1,0:T(8,128)(2,1)}) %reduce-scatter.11.cloned.1.call-update) | async-done | bytes 65552 | tf_op jit(solution)/shard_map/reduce_scatter | solution.py:351
  307.5 13.1 %psum.7 = f32[2176]{0:T(1024)S(1)} all-reduce(f32[2176]{0:T(1024)S(1)} %concatenate.47), channel_id=1, replica_groups=mesh['ctx'=32,'tp'=4] {'tp'}, use_global_device_ids=true, to_apply=%region_23.24 | all-reduce | flops 2176 | bytes 17408 | tf_op jit(solution)/shard_map/psum | solution.py:533
  321.2 220.9 %shard_map.239 = (bf16[1024,4224]{1,0:T(8,128)(2,1)}, f32[8,384]{1,0:T(8,128)}) custom-call(bf16[1024,4224]{1,0:T(8,128)(2,1)} %fusion.10.whole_ref, f32[8,384]{1,0:T(8,128)} %reshape.333.extra_ref), custom_call_target="tpu_custom_call" | custom-call | tf_op jit(solution)/shard_map/pallas_call | solution.py:250
  542.1 10.5 %convert_element_type.165 = f32[1024,4224]{1,0:T(8,128)} convert(bf16[1024,4224]{1,0:T(8,128)(2,1)} %get-tuple-element.16) | non-fusion elementwise | flops 4325376 | bytes 25952256 | tf_op jit(solution)/shard_map/convert_element_type | solution.py:541
  552.6 5.2 slice_bitcast_fusion
  557.8 1.7 slice_bitcast_fusion.1
  559.5 4.3 fusion.80
  565.0 2.1 slice.109
  567.1 6.2 %copy.103 = f32[1152,1024]{1,0:T(8,128)} copy(f32[1152,1024]{0,1:T(8,128)} %slice_bitcast_fusion) | data formatting | bytes 9437184
  575.2 2.1 fusion.81
  577.3 1.8 fusion.46
  (183 shorter events, 44.0 us)
Async XLA Ops:
  7.2 136.0 %copy-start = (bf16[1152,1024]{1,0:T(8,128)(2,1)S(1)}, bf16[1152,1024]{1,0:T(8,128)(2,1)}, u32[]{:S(2)}) copy-start(bf16[1152,1024]{1,0:T(8,128)(2,1)} %param.26) | copy-start | bytes 7077892
  7.2 123.7 %reduce-scatter.5.cloned.1.call-start = ((), (), s32[]{:S(2)}) async-start(), calls=%async_computation.4 | async-start | bytes 327680 | tf_op jit(solution)/shard_map/reduce_scatter | solution.py:351
  9.3 0.9 copy-start.49
  18.3 54.2 %copy-start.5 = (bf16[128,1024]{1,0:T(8,128)(2,1)}, bf16[128,1024]{1,0:T(8,128)(2,1)S(1)}, u32[]{:S(2)}) copy-start(bf16[128,1024]{1,0:T(8,128)(2,1)S(1)} %all_gather.12) | copy-start | bytes 786436
  19.7 52.8 %copy-start.29 = (f32[128,128]{0,1:T(8,128)}, f32[128,128]{0,1:T(8,128)S(1)}, u32[]{:S(2)}) copy-start(f32[128,128]{0,1:T(8,128)S(1)} %get-tuple-element.96) | copy-start | bytes 196612
  19.7 5.3 copy-start.46
  24.3 48.3 %copy-start.35 = (f32[128,32]{0,1:T(8,128)}, f32[128,32]{0,1:T(8,128)S(1)}, u32[]{:S(2)}) copy-start(f32[128,32]{0,1:T(8,128)S(1)} %get-tuple-element.94) | copy-start | bytes 49156
  77.0 16.9 %copy-start.17 = (f32[128,256]{0,1:T(8,128)}, f32[128,256]{0,1:T(8,128)S(1)}, u32[]{:S(2)}) copy-start(f32[128,256]{0,1:T(8,128)S(1)} %copy.78) | copy-start | bytes 393220
  77.1 2.1 copy-start.42
  91.9 3.2 copy-start.14
  91.9 3.2 copy-start.31
  94.0 3.2 copy-start.3
  94.0 3.2 copy-start.41
  95.1 2.0 copy-start.44
  95.1 7.5 %copy-start.33 = (bf16[32,1024]{1,0:T(8,128)(2,1)S(1)}, bf16[32,1024]{1,0:T(8,128)(2,1)}, u32[]{:S(2)}) copy-start(bf16[32,1024]{1,0:T(8,128)(2,1)} %param.27) | copy-start | bytes 196612
  95.1 35.8 %copy-start.11 = (bf16[32,1024]{1,0:T(8,128)(2,1)S(1)}, bf16[32,1024]{1,0:T(8,128)(2,1)}, u32[]{:S(2)}) copy-start(bf16[32,1024]{1,0:T(8,128)(2,1)} %param.14) | copy-start | bytes 196612
  102.6 71.4 %reduce-scatter.9.cloned.1.call-start = ((), (), s32[]{:S(2)}) async-start(), calls=%async_computation.6 | async-start | bytes 327680 | tf_op jit(solution)/shard_map/reduce_scatter | solution.py:351
  130.9 11.7 %copy-start.8 = (bf16[1024,1152]{1,0:T(8,128)(2,1)S(1)}, bf16[1024,1152]{1,0:T(8,128)(2,1)}, u32[]{:S(2)}) copy-start(bf16[1024,1152]{1,0:T(8,128)(2,1)} %param.25) | copy-start | bytes 7077892
  130.9 12.2 %copy-start.27 = (bf16[128,1024]{1,0:T(8,128)(2,1)S(1)}, bf16[128,1024]{1,0:T(8,128)(2,1)}, u32[]{:S(2)}) copy-start(bf16[128,1024]{1,0:T(8,128)(2,1)} %all_gather.14) | copy-start | bytes 786436
  132.1 10.5 %copy-start.47 = (f32[32]{0:T(128)}, f32[32]{0:T(128)S(1)}, u32[]{:S(2)}) copy-start(f32[32]{0:T(128)S(1)} %add_rsqrt_fusion.2) | copy-start | bytes 388
  140.3 2.3 copy-start.9
  142.6 2.3 copy-start.7
  144.9 0.9 copy-start.20
  144.9 0.9 copy-start.23
  144.9 29.0 %copy-start.19 = (bf16[32,1024]{1,0:T(8,128)(2,1)S(1)}, bf16[32,1024]{1,0:T(8,128)(2,1)}, u32[]{:S(2)}) copy-start(bf16[32,1024]{1,0:T(8,128)(2,1)} %reduce-scatter.5.cloned.1.call-done) | copy-start | bytes 196612
  147.4 158.9 %reduce-scatter.11.cloned.1.call-start = ((), (), s32[]{:S(2)}) async-start(), calls=%async_computation.7 | async-start | bytes 327680 | tf_op jit(solution)/shard_map/reduce_scatter | solution.py:351
  175.5 0.6 copy-start.53
  184.5 0.7 copy-start.12
  190.5 6.1 %copy-start.4 = (f32[2,2,2048,64,2]{2,3,4,1,0:T(8,128)S(1)}, f32[2,2,2048,64,2]{2,3,4,1,0:T(8,128)}, u32[]{:S(2)}) copy-start(f32[2,2,2048,64,2]{2,3,4,1,0:T(8,128)} %copy-done.3) | copy-start | bytes 12582916
  190.5 6.1 %copy-start.15 = (pred[64,2048]{1,0:T(8,128)(4,1)S(1)}, pred[64,2048]{1,0:T(8,128)(4,1)}, u32[]{:S(2)}) copy-start(pred[64,2048]{1,0:T(8,128)(4,1)} %copy-done.14) | copy-start | bytes 393220
  190.5 6.1 %copy-start.32 = (bf16[2,2048,128]{1,2,0:T(8,128)(2,1)S(1)}, bf16[2,2048,128]{1,2,0:T(8,128)(2,1)}, u32[]{:S(2)}) copy-start(bf16[2,2048,128]{1,2,0:T(8,128)(2,1)} %copy.81) | copy-start | bytes 3145732
  190.5 6.1 %copy-start.34 = (bf16[2,64,2,2,64]{1,4,3,2,0:T(8,128)(2,1)S(1)}, bf16[2,64,2,2,64]{1,4,3,2,0:T(8,128)(2,1)}, u32[]{:S(2)}) copy-start(bf16[2,64,2,2,64]{1,4,3,2,0:T(8,128)(2,1)} %copy.84) | copy-start | bytes 196612
  190.5 6.1 %copy-start.51 = (f32[2,2,2,64]{3,2,1,0:T(2,128)S(1)}, f32[2,2,2,64]{3,2,1,0:T(2,128)}, u32[]{:S(2)}) copy-start(f32[2,2,2,64]{3,2,1,0:T(2,128)} %log_add_fusion) | copy-start | bytes 6148
  196.6 1.8 copy-start.25
  196.6 1.8 copy-start.26
  215.6 49.4 %copy-start.36 = (f32[128,32]{0,1:T(8,128)S(1)}, f32[128,32]{0,1:T(8,128)}, u32[]{:S(2)}) copy-start(f32[128,32]{0,1:T(8,128)} %copy-done.35) | copy-start | bytes 49156
  215.6 49.4 %copy-start.30 = (f32[128,128]{0,1:T(8,128)S(1)}, f32[128,128]{0,1:T(8,128)}, u32[]{:S(2)}) copy-start(f32[128,128]{0,1:T(8,128)} %copy-done.29) | copy-start | bytes 196612
  215.6 49.5 %copy-start.52 = (f32[64]{0:T(128)S(1)}, f32[64]{0:T(128)}, u32[]{:S(2)}) copy-start(f32[64]{0:T(128)} %param.21) | copy-start | bytes 772
  215.6 53.7 %copy-start.18 = (f32[128,256]{0,1:T(8,128)S(1)}, f32[128,256]{0,1:T(8,128)}, u32[]{:S(2)}) copy-start(f32[128,256]{0,1:T(8,128)} %copy-done.17) | copy-start | bytes 393220
  215.6 53.7 %copy-start.48 = (f32[64]{0:T(128)S(1)}, f32[64]{0:T(128)}, u32[]{:S(2)}) copy-start(f32[64]{0:T(128)} %param.20) | copy-start | bytes 772
  215.6 58.3 %copy-start.21 = (f32[128,256]{1,0:T(8,128)S(1)}, f32[128,256]{1,0:T(8,128)}, u32[]{:S(2)}) copy-start(f32[128,256]{1,0:T(8,128)} %fusion.86) | copy-start | bytes 393220
  221.2 53.9 %copy-start.16 = (bf16[1024,256]{1,0:T(8,128)(2,1)S(1)}, bf16[1024,256]{1,0:T(8,128)(2,1)}, u32[]{:S(2)}) copy-start(bf16[1024,256]{1,0:T(8,128)(2,1)} %param.17) | copy-start | bytes 1572868
  270.0 12.4 %copy-start.6 = (bf16[128,1024]{1,0:T(8,128)(2,1)S(1)}, bf16[128,1024]{1,0:T(8,128)(2,1)}, u32[]{:S(2)}) copy-start(bf16[128,1024]{1,0:T(8,128)(2,1)} %copy-done.5) | copy-start | bytes 786436
  275.1 0.6 copy-start.38
  275.7 12.7 %copy-start.13 = (bf16[128,1024]{1,0:T(8,128)(2,1)S(1)}, bf16[128,1024]{1,0:T(8,128)(2,1)}, u32[]{:S(2)}) copy-start(bf16[128,1024]{1,0:T(8,128)(2,1)} %copy-done.12) | copy-start | bytes 786436
  276.7 5.7 copy-start.37
  276.7 13.7 %copy-start.10 = (bf16[128,1024]{1,0:T(8,128)(2,1)S(1)}, bf16[128,1024]{1,0:T(8,128)(2,1)}, u32[]{:S(2)}) copy-start(bf16[128,1024]{1,0:T(8,128)(2,1)} %copy-done.9) | copy-start | bytes 786436
  279.9 297.3 %reduce-scatter.7.cloned.1.call-start = ((), (), s32[]{:S(2)}) async-start(), calls=%async_computation.5 | async-start | bytes 327680 | tf_op jit(solution)/shard_map/reduce_scatter | solution.py:351
  282.4 11.3 %copy-start.24 = (bf16[128,1152]{1,0:T(8,128)(2,1)S(1)}, bf16[128,1152]{1,0:T(8,128)(2,1)}, u32[]{:S(2)}) copy-start(bf16[128,1152]{1,0:T(8,128)(2,1)} %copy-done.23) | copy-start | bytes 884740
  282.4 13.6 %copy-start.22 = (bf16[128,1152]{1,0:T(8,128)(2,1)S(1)}, bf16[128,1152]{1,0:T(8,128)(2,1)}, u32[]{:S(2)}) copy-start(bf16[128,1152]{1,0:T(8,128)(2,1)} %get-tuple-element.70) | copy-start | bytes 884740
  282.4 13.5 %copy-start.28 = (bf16[128,1024]{1,0:T(8,128)(2,1)S(1)}, bf16[128,1024]{1,0:T(8,128)(2,1)}, u32[]{:S(2)}) copy-start(bf16[128,1024]{1,0:T(8,128)(2,1)} %all_gather.14) | copy-start | bytes 786436
  290.4 16.0 %copy-start.40 = (f32[1024]{0:T(1024)S(1)}, f32[1024]{0:T(1024)}, u32[]{:S(2)}) copy-start(f32[1024]{0:T(1024)} %param.16) | copy-start | bytes 12292
  290.4 16.0 %copy-start.50 = (f32[32]{0:T(128)S(1)}, f32[32]{0:T(128)}, u32[]{:S(2)}) copy-start(f32[32]{0:T(128)} %copy-done.49) | copy-start | bytes 388
  290.4 17.0 %copy-start.43 = (f32[1024]{0:T(1024)S(1)}, f32[1024]{0:T(1024)}, u32[]{:S(2)}) copy-start(f32[1024]{0:T(1024)} %get-tuple-element.56) | copy-start | bytes 12292
  552.6 6.9 %copy-start.2 = (bf16[1024,4224]{1,0:T(8,128)(2,1)S(1)}, bf16[1024,4224]{1,0:T(8,128)(2,1)}, u32[]{:S(2)}) copy-start(bf16[1024,4224]{1,0:T(8,128)(2,1)} %get-tuple-element.16) | copy-start | bytes 25952260
  559.5 4.4 copy-start.45
  567.1 11.9 %copy-start.1 = (bf16[1152,1024]{1,0:T(8,128)(2,1)S(1)}, bf16[1152,1024]{1,0:T(8,128)(2,1)}, u32[]{:S(2)}) copy-start(bf16[1152,1024]{1,0:T(8,128)(2,1)} %param.26) | copy-start | bytes 7077892
  573.3 4.0 copy-start.39
Sparse Core Ops, SparseCore 0:
  102.7 28.2 reduce-scatter.4
  147.6 26.3 reduce-scatter.8
  280.0 26.2 reduce-scatter.10
  309.0 53.0 reduce-scatter.6
where the time goes:
time: 588 us; the launch traced here: 586 us
  Pallas kernels  306 us (52%)
  local copies, waits for them, and re-layouts  79.4 us (14%)
  matrix products  50.9 us (9%)
  waiting for transfers between devices  45.6 us (8%)
  other arithmetic  44.3 us (8%)
  blocking collectives  44 us (7%)
  between operations  15.1 us (3%)
    pallas_call x1, Pallas kernels, ctx_sum(): pl.pallas_call(functools.partial(_sum_kernel, n, spans), out_shape=(jax.S...  221 us
    reduce_scatter x4, waiting for transfers between devices, reduce_rows(): lax.psum_scatter(partial_rows.astype(jnp.bfloat16), 'tp', scatter_dimensi...  45.5 us
    pallas_call x1, Pallas kernels, ctx_scatter(): pl.pallas_call(functools.partial(_scatter_kernel, n), out_shape=jax.Shape...  42.9 us
    pallas_call x1, Pallas kernels, ctx_gather(): pl.pallas_call(functools.partial(_gather_kernel, n), out_shape=jax.ShapeD...  42.1 us
    all_gather x4, blocking collectives, gather_rows(): return lax.all_gather(rows_low, 'tp', axis=0, tiled=True)  30.9 us
    psum x1, blocking collectives, per_device(): gain_flat = lax.psum(jnp.concatenate(gain_parts), 'tp')  13.1 us
  transfers between devices with their start and end apart: 4, of which 3 were waited for; matrix products, arithmetic and copies ran while one was open for 11% of the time, Pallas kernels for 38%

commit v1 on v0

--- a/solution.py
+++ b/solution.py
@@ -21,6 +21,11 @@
     return order
 
 
+def _shift_at(n, step):
+    half = step // 2 + 1
+    return jnp.where(step % 2 == 0, half, n - half)
+
+
 def _enter(n, me, peer_axis):
     barrier = pltpu.get_barrier_semaphore()
     for k in _shifts(n):
@@ -35,31 +40,33 @@
     other = lax.axis_index("tp")
     rows = part_ref.shape[0]
     _enter(n, me, other)
-    copies = []
-    for k in _shifts(n):
-        copy = pltpu.make_async_remote_copy(
+
+    def block_copy(k, peer, block):
+        return pltpu.make_async_remote_copy(
             src_ref=part_ref,
-            dst_ref=out_ref.at[pl.ds(pl.multiple_of(me * rows, rows), rows)],
+            dst_ref=out_ref.at[pl.ds(pl.multiple_of(block * rows, rows), rows)],
             send_sem=send_sem.at[k],
             recv_sem=recv_sem.at[k],
-            device_id=(lax.rem(me + k, n), other),
+            device_id=(peer, other),
             device_id_type=MESH,
         )
-        copy.start()
-        copies.append(copy)
+
+    def start(index, carry):
+        k = _shift_at(n, index)
+        block_copy(k, lax.rem(me + k, n), me).start()
+        return carry
+
+    lax.fori_loop(0, n - 1, start, 0)
     out_ref[pl.ds(pl.multiple_of(me * rows, rows), rows), :] = part_ref[...]
-    for k in _shifts(n):
+
+    def finish(index, carry):
+        k = _shift_at(n, index)
         source = lax.rem(me + n - k, n)
-        pltpu.make_async_remote_copy(
-            src_ref=part_ref,
-            dst_ref=out_ref.at[pl.ds(pl.multiple_of(source * rows, rows), rows)],
-            send_sem=send_sem.at[k],
-            recv_sem=recv_sem.at[k],
-            device_id=(source, other),
-            device_id_type=MESH,
-        ).wait_recv()
-    for copy in copies:
-        copy.wait_send()
+        block_copy(k, source, source).wait_recv()
+        block_copy(k, lax.rem(me + k, n), me).wait_send()
+        return carry
+
+    lax.fori_loop(0, n - 1, finish, 0)
 
 
 def ctx_gather(part, n, collective_id):
@@ -77,33 +84,43 @@
 
 
 def _scatter_sum(n, me, other, whole_ref, held, send_sem, recv_sem, rows):
-    copies = []
-    for k in _shifts(n):
-        target = lax.rem(me + k, n)
-        copy = pltpu.make_async_remote_copy(
-            src_ref=whole_ref.at[pl.ds(pl.multiple_of(target * rows, rows), rows)],
+    def block_copy(k, peer, block):
+        return pltpu.make_async_remote_copy(
+            src_ref=whole_ref.at[pl.ds(pl.multiple_of(block * rows, rows), rows)],
             dst_ref=held.at[k],
             send_sem=send_sem.at[k],
             recv_sem=recv_sem.at[k],
-            device_id=(target, other),
+            device_id=(peer, other),
             device_id_type=MESH,
         )
-        copy.start()
-        copies.append(copy)
-    total = whole_ref[pl.ds(pl.multiple_of(me * rows, rows), rows), :].astype(jnp.float32)
-    for k in _shifts(n):
-        source = lax.rem(me + n - k, n)
-        pltpu.make_async_remote_copy(
-            src_ref=whole_ref.at[pl.ds(0, rows)],
-            dst_ref=held.at[k],
-            send_sem=send_sem.at[k],
-            recv_sem=recv_sem.at[k],
-            device_id=(source, other),
-            device_id_type=MESH,
-        ).wait_recv()
-        total = total + held[k].astype(jnp.float32)
-    for copy in copies:
-        copy.wait_send()
+
+    def start(index, carry):
+        k = _shift_at(n, index)
+        target = lax.rem(me + k, n)
+        block_copy(k, target, target).start()
+        return carry
+
+    lax.fori_loop(0, n - 1, start, 0)
+
+    def add_block(index, total):
+        k = _shift_at(n, index)
+        block_copy(k, lax.rem(me + n - k, n), me).wait_recv()
+        return total + held[k].astype(jnp.float32)
+
+    total = lax.fori_loop(
+        0,
+        n - 1,
+        add_block,
+        whole_ref[pl.ds(pl.multiple_of(me * rows, rows), rows), :].astype(jnp.float32),
+    )
+
+    def finish(index, carry):
+        k = _shift_at(n, index)
+        target = lax.rem(me + k, n)
+        block_copy(k, target, target).wait_send()
+        return carry
+
+    lax.fori_loop(0, n - 1, finish, 0)
     return total
 
 
@@ -131,11 +148,6 @@
             collective_id=collective_id, has_side_effects=True, vmem_limit_bytes=VMEM_LIMIT
         ),
     )(whole)
-
-
-def _shift_at(n, step):
-    half = step // 2 + 1
-    return jnp.where(step % 2 == 0, half, n - half)
 
 
 def _sum_kernel(n, spans, whole_ref, extra_ref, out_ref, extra_out, *scratch):

time: 588 us -> 592 us (level)
  the two profiles are of different devices: /device:TPU:28 before, /device:TPU:68 now
where the time goes in v1:
time: 592 us; the launch traced here: 590 us
  Pallas kernels  305 us (52%)
  local copies, waits for them, and re-layouts  79.4 us (13%)
  matrix products  50.9 us (9%)
  waiting for transfers between devices  49.6 us (8%)
  blocking collectives  45.5 us (8%)
  other arithmetic  44.3 us (7%)
  between operations  15.1 us (3%)
    pallas_call x1, Pallas kernels, ctx_sum(): pl.pallas_call(functools.partial(_sum_kernel, n, spans), out_shape=(jax.S...  226 us
    reduce_scatter x4, waiting for transfers between devices, reduce_rows(): lax.psum_scatter(partial_rows.astype(jnp.bfloat16), 'tp', scatter_dimensi...  49.5 us
    pallas_call x1, Pallas kernels, ctx_scatter(): pl.pallas_call(functools.partial(_scatter_kernel, n), out_shape=jax.Shape...  39.5 us
    pallas_call x1, Pallas kernels, ctx_gather(): pl.pallas_call(functools.partial(_gather_kernel, n), out_shape=jax.ShapeD...  39.3 us
    all_gather x4, blocking collectives, gather_rows(): return lax.all_gather(rows_low, 'tp', axis=0, tiled=True)  30 us
    psum x1, blocking collectives, per_device(): gain_flat = lax.psum(jnp.concatenate(gain_parts), 'tp')  15.4 us
  transfers between devices with their start and end apart: 4, of which 3 were waited for; matrix products, arithmetic and copies ran while one was open for 11% of the time, Pallas kernels for 38%

profile of v1, /device:TPU:68, one launch (start us, length us, event | category | flops | bytes accessed | tf_op | source)
XLA Modules:
  0.0 590.1 jit_solution(17630158357126501097)
XLA Ops:
  10.2 7.3 %all_gather.12 = bf16[128,1024]{1,0:T(8,128)(2,1)S(1)} all-gather(bf16[32,1024]{1,0:T(8,128)(2,1)S(1)} %fusion.43), channel_id=1, replica_groups=mesh['ctx'=32,'tp'=4] {'tp'}, dimensions={0}, use_global_device_ids=true | all-gather | bytes 327680 | tf_op jit(solution)/shard_map/all_gather | solution.py:359
  26.1 39.3 %shard_map.237 = bf16[4096,256]{1,0:T(8,128)(2,1)} custom-call(bf16[128,256]{1,0:T(8,128)(2,1)} %pad_maximum_fusion.2.part_ref), custom_call_target="tpu_custom_call" | custom-call | tf_op jit(solution)/shard_map/pallas_call | solution.py:74
  65.4 1.7 copy.76
  67.2 1.7 fusion.82
  68.9 1.5 copy.77
  70.4 2.0 fusion.86
  74.2 1.4 subtract_convert_fusion
  75.5 1.5 concatenate.38
  77.0 1.6 copy.79
  78.6 1.5 concatenate.39
  80.1 1.6 copy.80
  82.4 1.4 multiply_add_fusion.2
  83.8 1.4 add.168
  85.1 2.3 copy.81
  88.3 2.0 fusion.2
  91.5 2.0 fusion.85
  93.5 1.7 copy.82
  95.2 1.7 convert_element_type.134
  96.9 2.0 convolution_convert_fusion.8
  99.0 7.7 %all_gather.14 = bf16[128,1024]{1,0:T(8,128)(2,1)} all-gather(bf16[32,1024]{1,0:T(8,128)(2,1)S(1)} %copy-done.33), channel_id=1, replica_groups=mesh['ctx'=32,'tp'=4] {'tp'}, dimensions={0}, use_global_device_ids=true | all-gather | bytes 327680 | tf_op jit(solution)/shard_map/all_gather | solution.py:359
  106.7 21.0 %reduce-scatter.5.cloned.1.call-done = bf16[32,1024]{1,0:T(8,128)(2,1)} async-done(((bf16[128,1024]{1,0:T(8,128)(2,1)}), bf16[32,1024]{1,0:T(8,128)(2,1)}) %reduce-scatter.5.cloned.1.call-update) | async-done | bytes 65552 | tf_op jit(solution)/shard_map/reduce_scatter | solution.py:363
  129.7 7.4 %all_gather.13 = bf16[128,1024]{1,0:T(8,128)(2,1)S(1)} all-gather(bf16[32,1024]{1,0:T(8,128)(2,1)S(1)} %multiply_convert_fusion.3), channel_id=1, replica_groups=mesh['ctx'=32,'tp'=4] {'tp'}, dimensions={0}, use_global_device_ids=true | all-gather | bytes 327680 | tf_op jit(solution)/shard_map/all_gather | solution.py:359
  137.2 2.3 fusion.87
  140.0 1.7 multiply_convert_fusion
  142.7 1.6 fusion.31
  148.2 1.6 copy.90
  153.7 17.0 %reduce-scatter.9.cloned.1.call-done = bf16[32,1024]{1,0:T(8,128)(2,1)} async-done(((bf16[128,1024]{1,0:T(8,128)(2,1)}), bf16[32,1024]{1,0:T(8,128)(2,1)}) %reduce-scatter.9.cloned.1.call-update) | async-done | bytes 65552 | tf_op jit(solution)/shard_map/reduce_scatter | solution.py:363
  170.7 1.5 fusion.51
  173.8 7.6 %all_gather.15 = bf16[128,1024]{1,0:T(8,128)(2,1)S(1)} all-gather(bf16[32,1024]{1,0:T(8,128)(2,1)S(1)} %fusion.77), channel_id=1, replica_groups=mesh['ctx'=32,'tp'=4] {'tp'}, dimensions={0}, use_global_device_ids=true | all-gather | bytes 327680 | tf_op jit(solution)/shard_map/all_gather | solution.py:359
  182.1 2.0 convolution_convert_fusion.9
  184.0 1.6 reshape.328
  185.7 1.7 copy.84
  188.5 4.9 fusion.16
  193.5 1.7 fusion.1
  195.3 1.5 fusion.17
  196.8 1.8 convolution_bitcast_fusion.2
  198.6 4.4 reshape.330
  203.0 4.4 reshape.331
  207.4 5.0 maximum_bitcast_fusion
  212.5 5.5 copy.93
  218.0 39.5 %shard_map.238 = f32[128,256]{1,0:T(8,128)} custom-call(bf16[4096,256]{1,0:T(8,128)(2,1)} %bitcast.191), custom_call_target="tpu_custom_call" | custom-call | tf_op jit(solution)/shard_map/pallas_call | solution.py:137
  259.7 1.9 copy.85
  264.1 1.7 copy.89
  265.8 1.7 copy.86
  271.4 1.9 fusion.28
  273.6 2.2 convolution_convert_fusion.7
  275.9 2.1 fusion.27
  278.2 1.8 fusion.30
  280.0 1.9 fusion.29
  281.8 2.0 fusion.26
  283.9 3.3 fusion.8
  287.1 2.3 fusion.7
  289.4 2.4 fusion.10.whole_ref
  291.8 11.6 %reduce-scatter.11.cloned.1.call-done = bf16[32,1024]{1,0:T(8,128)(2,1)} async-done(((bf16[128,1024]{1,0:T(8,128)(2,1)}), bf16[32,1024]{1,0:T(8,128)(2,1)}) %reduce-scatter.11.cloned.1.call-update) | async-done | bytes 65552 | tf_op jit(solution)/shard_map/reduce_scatter | solution.py:363
  304.5 15.4 %psum.7 = f32[2176]{0:T(1024)S(1)} all-reduce(f32[2176]{0:T(1024)S(1)} %concatenate.47), channel_id=1, replica_groups=mesh['ctx'=32,'tp'=4] {'tp'}, use_global_device_ids=true, to_apply=%region_23.24 | all-reduce | flops 2176 | bytes 17408 | tf_op jit(solution)/shard_map/psum | solution.py:545
  320.5 226.1 %shard_map.239 = (bf16[1024,4224]{1,0:T(8,128)(2,1)}, f32[8,384]{1,0:T(8,128)}) custom-call(bf16[1024,4224]{1,0:T(8,128)(2,1)} %fusion.10.whole_ref, f32[8,384]{1,0:T(8,128)} %reshape.333.extra_ref), custom_call_target="tpu_custom_call" | custom-call | tf_op jit(solution)/shard_map/pallas_call | solution.py:262
  546.6 10.5 %convert_element_type.165 = f32[1024,4224]{1,0:T(8,128)} convert(bf16[1024,4224]{1,0:T(8,128)(2,1)} %get-tuple-element.16) | non-fusion elementwise | flops 4325376 | bytes 25952256 | tf_op jit(solution)/shard_map/convert_element_type | solution.py:553
  557.1 5.2 slice_bitcast_fusion
  562.3 1.7 slice_bitcast_fusion.1
  564.0 4.3 fusion.80
  569.5 2.1 slice.109
  571.6 6.2 %copy.103 = f32[1152,1024]{1,0:T(8,128)} copy(f32[1152,1024]{0,1:T(8,128)} %slice_bitcast_fusion) | data formatting | bytes 9437184
  579.7 2.1 fusion.81
  581.8 1.8 fusion.46
  (183 shorter events, 44.0 us)
Async XLA Ops:
  7.2 132.8 %copy-start = (bf16[1152,1024]{1,0:T(8,128)(2,1)S(1)}, bf16[1152,1024]{1,0:T(8,128)(2,1)}, u32[]{:S(2)}) copy-start(bf16[1152,1024]{1,0:T(8,128)(2,1)} %param.26) | copy-start | bytes 7077892
  7.2 120.5 %reduce-scatter.5.cloned.1.call-start = ((), (), s32[]{:S(2)}) async-start(), calls=%async_computation.4 | async-start | bytes 327680 | tf_op jit(solution)/shard_map/reduce_scatter | solution.py:363
  9.3 0.9 copy-start.49
  17.5 51.4 %copy-start.5 = (bf16[128,1024]{1,0:T(8,128)(2,1)}, bf16[128,1024]{1,0:T(8,128)(2,1)S(1)}, u32[]{:S(2)}) copy-start(bf16[128,1024]{1,0:T(8,128)(2,1)S(1)} %all_gather.12) | copy-start | bytes 786436
  18.8 50.0 %copy-start.29 = (f32[128,128]{0,1:T(8,128)}, f32[128,128]{0,1:T(8,128)S(1)}, u32[]{:S(2)}) copy-start(f32[128,128]{0,1:T(8,128)S(1)} %get-tuple-element.96) | copy-start | bytes 196612
  18.9 5.3 copy-start.46
  23.4 45.4 %copy-start.35 = (f32[128,32]{0,1:T(8,128)}, f32[128,32]{0,1:T(8,128)S(1)}, u32[]{:S(2)}) copy-start(f32[128,32]{0,1:T(8,128)S(1)} %get-tuple-element.94) | copy-start | bytes 49156
  73.4 16.9 %copy-start.17 = (f32[128,256]{0,1:T(8,128)}, f32[128,256]{0,1:T(8,128)S(1)}, u32[]{:S(2)}) copy-start(f32[128,256]{0,1:T(8,128)S(1)} %copy.78) | copy-start | bytes 393220
  73.4 2.1 copy-start.42
  88.2 3.2 copy-start.14
  88.3 3.2 copy-start.31
  90.3 3.2 copy-start.3
  90.3 3.2 copy-start.41
  91.5 2.0 copy-start.44
  91.5 7.5 %copy-start.33 = (bf16[32,1024]{1,0:T(8,128)(2,1)S(1)}, bf16[32,1024]{1,0:T(8,128)(2,1)}, u32[]{:S(2)}) copy-start(bf16[32,1024]{1,0:T(8,128)(2,1)} %param.27) | copy-start | bytes 196612
  91.5 36.2 %copy-start.11 = (bf16[32,1024]{1,0:T(8,128)(2,1)S(1)}, bf16[32,1024]{1,0:T(8,128)(2,1)}, u32[]{:S(2)}) copy-start(bf16[32,1024]{1,0:T(8,128)(2,1)} %param.14) | copy-start | bytes 196612
  98.9 71.8 %reduce-scatter.9.cloned.1.call-start = ((), (), s32[]{:S(2)}) async-start(), calls=%async_computation.6 | async-start | bytes 327680 | tf_op jit(solution)/shard_map/reduce_scatter | solution.py:363
  127.7 11.8 %copy-start.8 = (bf16[1024,1152]{1,0:T(8,128)(2,1)S(1)}, bf16[1024,1152]{1,0:T(8,128)(2,1)}, u32[]{:S(2)}) copy-start(bf16[1024,1152]{1,0:T(8,128)(2,1)} %param.25) | copy-start | bytes 7077892
  127.7 12.4 %copy-start.27 = (bf16[128,1024]{1,0:T(8,128)(2,1)S(1)}, bf16[128,1024]{1,0:T(8,128)(2,1)}, u32[]{:S(2)}) copy-start(bf16[128,1024]{1,0:T(8,128)(2,1)} %all_gather.14) | copy-start | bytes 786436
  128.8 10.6 %copy-start.47 = (f32[32]{0:T(128)}, f32[32]{0:T(128)S(1)}, u32[]{:S(2)}) copy-start(f32[32]{0:T(128)S(1)} %add_rsqrt_fusion.2) | copy-start | bytes 388
  137.2 2.3 copy-start.9
  139.5 2.3 copy-start.7
  141.7 0.9 copy-start.20
  141.7 0.9 copy-start.23
  141.7 28.9 %copy-start.19 = (bf16[32,1024]{1,0:T(8,128)(2,1)S(1)}, bf16[32,1024]{1,0:T(8,128)(2,1)}, u32[]{:S(2)}) copy-start(bf16[32,1024]{1,0:T(8,128)(2,1)} %reduce-scatter.5.cloned.1.call-done) | copy-start | bytes 196612
  144.3 159.1 %reduce-scatter.11.cloned.1.call-start = ((), (), s32[]{:S(2)}) async-start(), calls=%async_computation.7 | async-start | bytes 327680 | tf_op jit(solution)/shard_map/reduce_scatter | solution.py:363
  172.2 0.6 copy-start.53
  181.4 0.7 copy-start.12
  187.3 6.1 %copy-start.4 = (f32[2,2,2048,64,2]{2,3,4,1,0:T(8,128)S(1)}, f32[2,2,2048,64,2]{2,3,4,1,0:T(8,128)}, u32[]{:S(2)}) copy-start(f32[2,2,2048,64,2]{2,3,4,1,0:T(8,128)} %copy-done.3) | copy-start | bytes 12582916
  187.3 6.1 %copy-start.15 = (pred[64,2048]{1,0:T(8,128)(4,1)S(1)}, pred[64,2048]{1,0:T(8,128)(4,1)}, u32[]{:S(2)}) copy-start(pred[64,2048]{1,0:T(8,128)(4,1)} %copy-done.14) | copy-start | bytes 393220
  187.3 6.1 %copy-start.32 = (bf16[2,2048,128]{1,2,0:T(8,128)(2,1)S(1)}, bf16[2,2048,128]{1,2,0:T(8,128)(2,1)}, u32[]{:S(2)}) copy-start(bf16[2,2048,128]{1,2,0:T(8,128)(2,1)} %copy.81) | copy-start | bytes 3145732
  187.3 6.1 %copy-start.34 = (bf16[2,64,2,2,64]{1,4,3,2,0:T(8,128)(2,1)S(1)}, bf16[2,64,2,2,64]{1,4,3,2,0:T(8,128)(2,1)}, u32[]{:S(2)}) copy-start(bf16[2,64,2,2,64]{1,4,3,2,0:T(8,128)(2,1)} %copy.84) | copy-start | bytes 196612
  187.3 6.1 %copy-start.51 = (f32[2,2,2,64]{3,2,1,0:T(2,128)S(1)}, f32[2,2,2,64]{3,2,1,0:T(2,128)}, u32[]{:S(2)}) copy-start(f32[2,2,2,64]{3,2,1,0:T(2,128)} %log_add_fusion) | copy-start | bytes 6148
  193.5 1.8 copy-start.25
  193.5 1.8 copy-start.26
  212.5 46.0 %copy-start.36 = (f32[128,32]{0,1:T(8,128)S(1)}, f32[128,32]{0,1:T(8,128)}, u32[]{:S(2)}) copy-start(f32[128,32]{0,1:T(8,128)} %copy-done.35) | copy-start | bytes 49156
  212.5 46.0 %copy-start.30 = (f32[128,128]{0,1:T(8,128)S(1)}, f32[128,128]{0,1:T(8,128)}, u32[]{:S(2)}) copy-start(f32[128,128]{0,1:T(8,128)} %copy-done.29) | copy-start | bytes 196612
  212.5 46.1 %copy-start.52 = (f32[64]{0:T(128)S(1)}, f32[64]{0:T(128)}, u32[]{:S(2)}) copy-start(f32[64]{0:T(128)} %param.21) | copy-start | bytes 772
  212.5 50.3 %copy-start.18 = (f32[128,256]{0,1:T(8,128)S(1)}, f32[128,256]{0,1:T(8,128)}, u32[]{:S(2)}) copy-start(f32[128,256]{0,1:T(8,128)} %copy-done.17) | copy-start | bytes 393220
  212.5 50.3 %copy-start.48 = (f32[64]{0:T(128)S(1)}, f32[64]{0:T(128)}, u32[]{:S(2)}) copy-start(f32[64]{0:T(128)} %param.20) | copy-start | bytes 772
  212.5 54.9 %copy-start.21 = (f32[128,256]{1,0:T(8,128)S(1)}, f32[128,256]{1,0:T(8,128)}, u32[]{:S(2)}) copy-start(f32[128,256]{1,0:T(8,128)} %fusion.86) | copy-start | bytes 393220
  218.0 50.5 %copy-start.16 = (bf16[1024,256]{1,0:T(8,128)(2,1)S(1)}, bf16[1024,256]{1,0:T(8,128)(2,1)}, u32[]{:S(2)}) copy-start(bf16[1024,256]{1,0:T(8,128)(2,1)} %param.17) | copy-start | bytes 1572868
  263.4 12.4 %copy-start.6 = (bf16[128,1024]{1,0:T(8,128)(2,1)S(1)}, bf16[128,1024]{1,0:T(8,128)(2,1)}, u32[]{:S(2)}) copy-start(bf16[128,1024]{1,0:T(8,128)(2,1)} %copy-done.5) | copy-start | bytes 786436
  268.5 0.6 copy-start.38
  269.2 12.7 %copy-start.13 = (bf16[128,1024]{1,0:T(8,128)(2,1)S(1)}, bf16[128,1024]{1,0:T(8,128)(2,1)}, u32[]{:S(2)}) copy-start(bf16[128,1024]{1,0:T(8,128)(2,1)} %copy-done.12) | copy-start | bytes 786436
  270.2 5.7 copy-start.37
  270.2 13.7 %copy-start.10 = (bf16[128,1024]{1,0:T(8,128)(2,1)S(1)}, bf16[128,1024]{1,0:T(8,128)(2,1)}, u32[]{:S(2)}) copy-start(bf16[128,1024]{1,0:T(8,128)(2,1)} %copy-done.9) | copy-start | bytes 786436
  273.4 308.4 %reduce-scatter.7.cloned.1.call-start = ((), (), s32[]{:S(2)}) async-start(), calls=%async_computation.5 | async-start | bytes 327680 | tf_op jit(solution)/shard_map/reduce_scatter | solution.py:363
  275.8 11.3 %copy-start.24 = (bf16[128,1152]{1,0:T(8,128)(2,1)S(1)}, bf16[128,1152]{1,0:T(8,128)(2,1)}, u32[]{:S(2)}) copy-start(bf16[128,1152]{1,0:T(8,128)(2,1)} %copy-done.23) | copy-start | bytes 884740
  275.9 13.6 %copy-start.22 = (bf16[128,1152]{1,0:T(8,128)(2,1)S(1)}, bf16[128,1152]{1,0:T(8,128)(2,1)}, u32[]{:S(2)}) copy-start(bf16[128,1152]{1,0:T(8,128)(2,1)} %get-tuple-element.70) | copy-start | bytes 884740
  275.9 13.5 %copy-start.28 = (bf16[128,1024]{1,0:T(8,128)(2,1)S(1)}, bf16[128,1024]{1,0:T(8,128)(2,1)}, u32[]{:S(2)}) copy-start(bf16[128,1024]{1,0:T(8,128)(2,1)} %all_gather.14) | copy-start | bytes 786436
  283.9 19.5 %copy-start.40 = (f32[1024]{0:T(1024)S(1)}, f32[1024]{0:T(1024)}, u32[]{:S(2)}) copy-start(f32[1024]{0:T(1024)} %param.16) | copy-start | bytes 12292
  283.9 19.5 %copy-start.50 = (f32[32]{0:T(128)S(1)}, f32[32]{0:T(128)}, u32[]{:S(2)}) copy-start(f32[32]{0:T(128)} %copy-done.49) | copy-start | bytes 388
  283.9 20.5 %copy-start.43 = (f32[1024]{0:T(1024)S(1)}, f32[1024]{0:T(1024)}, u32[]{:S(2)}) copy-start(f32[1024]{0:T(1024)} %get-tuple-element.56) | copy-start | bytes 12292
  557.1 6.9 %copy-start.2 = (bf16[1024,4224]{1,0:T(8,128)(2,1)S(1)}, bf16[1024,4224]{1,0:T(8,128)(2,1)}, u32[]{:S(2)}) copy-start(bf16[1024,4224]{1,0:T(8,128)(2,1)} %get-tuple-element.16) | copy-start | bytes 25952260
  564.0 4.4 copy-start.45
  571.6 11.9 %copy-start.1 = (bf16[1152,1024]{1,0:T(8,128)(2,1)S(1)}, bf16[1152,1024]{1,0:T(8,128)(2,1)}, u32[]{:S(2)}) copy-start(bf16[1152,1024]{1,0:T(8,128)(2,1)} %param.26) | copy-start | bytes 7077892
  577.8 4.0 copy-start.39
Sparse Core Ops, SparseCore 0:
  99.0 28.5 reduce-scatter.4
  144.4 26.2 reduce-scatter.8
  273.5 29.8 reduce-scatter.10
  305.9 67.4 reduce-scatter.6

commit v2 on v0

--- a/solution.py
+++ b/solution.py
@@ -242,7 +242,7 @@
     each_peer(finish_extra)
 
 
-def ctx_sum(whole, extra, n, collective_id, pieces=8):
+def ctx_sum(whole, extra, n, collective_id, pieces=11):
     rows, cols = whole.shape[0] // n, whole.shape[1]
     lanes = cols // 128
     edges = [128 * (lanes * p // pieces) for p in range(pieces + 1)]

time: 588 us -> 604 us (1.027)
  the two profiles are of different devices: /device:TPU:28 before, /device:TPU:68 now
where the time goes in v2:
time: 604 us; the launch traced here: 602 us
  Pallas kernels  317 us (52%)
  local copies, waits for them, and re-layouts  79.4 us (13%)
  matrix products  50.9 us (8%)
  waiting for transfers between devices  49.6 us (8%)
  blocking collectives  45.5 us (8%)
  other arithmetic  44.3 us (7%)
  between operations  15.1 us (2%)
    pallas_call x1, Pallas kernels, ctx_sum(): pl.pallas_call(functools.partial(_sum_kernel, n, spans), out_shape=(jax.S...  238 us
    reduce_scatter x4, waiting for transfers between devices, reduce_rows(): lax.psum_scatter(partial_rows.astype(jnp.bfloat16), 'tp', scatter_dimensi...  49.6 us
    pallas_call x1, Pallas kernels, ctx_gather(): pl.pallas_call(functools.partial(_gather_kernel, n), out_shape=jax.ShapeD...  39.3 us
    pallas_call x1, Pallas kernels, ctx_scatter(): pl.pallas_call(functools.partial(_scatter_kernel, n), out_shape=jax.Shape...  39.2 us
    all_gather x4, blocking collectives, gather_rows(): return lax.all_gather(rows_low, 'tp', axis=0, tiled=True)  30 us
    psum x1, blocking collectives, per_device(): gain_flat = lax.psum(jnp.concatenate(gain_parts), 'tp')  15.5 us
  transfers between devices with their start and end apart: 4, of which 3 were waited for; matrix products, arithmetic and copies ran while one was open for 11% of the time, Pallas kernels for 40%

profile of v2, /device:TPU:68, one launch (start us, length us, event | category | flops | bytes accessed | tf_op | source)
XLA Modules:
  0.0 601.7 jit_solution(10989265728479136556)
XLA Ops:
  10.2 7.3 %all_gather.12 = bf16[128,1024]{1,0:T(8,128)(2,1)S(1)} all-gather(bf16[32,1024]{1,0:T(8,128)(2,1)S(1)} %fusion.43), channel_id=1, replica_groups=mesh['ctx'=32,'tp'=4] {'tp'}, dimensions={0}, use_global_device_ids=true | all-gather | bytes 327680 | tf_op jit(solution)/shard_map/all_gather | solution.py:347
  26.1 39.3 %shard_map.237 = bf16[4096,256]{1,0:T(8,128)(2,1)} custom-call(bf16[128,256]{1,0:T(8,128)(2,1)} %pad_maximum_fusion.2.part_ref), custom_call_target="tpu_custom_call" | custom-call | tf_op jit(solution)/shard_map/pallas_call | solution.py:67
  65.5 1.7 copy.76
  67.2 1.7 fusion.82
  68.9 1.5 copy.77
  70.4 2.0 fusion.86
  74.2 1.4 subtract_convert_fusion
  75.6 1.5 concatenate.38
  77.1 1.6 copy.79
  78.7 1.5 concatenate.39
  80.2 1.6 copy.80
  82.4 1.4 multiply_add_fusion.2
  83.8 1.4 add.168
  85.2 2.3 copy.81
  88.3 2.0 fusion.2
  91.5 2.0 fusion.85
  93.5 1.7 copy.82
  95.2 1.7 convert_element_type.134
  96.9 2.0 convolution_convert_fusion.8
  99.0 7.7 %all_gather.14 = bf16[128,1024]{1,0:T(8,128)(2,1)} all-gather(bf16[32,1024]{1,0:T(8,128)(2,1)S(1)} %copy-done.33), channel_id=1, replica_groups=mesh['ctx'=32,'tp'=4] {'tp'}, dimensions={0}, use_global_device_ids=true | all-gather | bytes 327680 | tf_op jit(solution)/shard_map/all_gather | solution.py:347
  106.7 21.0 %reduce-scatter.5.cloned.1.call-done = bf16[32,1024]{1,0:T(8,128)(2,1)} async-done(((bf16[128,1024]{1,0:T(8,128)(2,1)}), bf16[32,1024]{1,0:T(8,128)(2,1)}) %reduce-scatter.5.cloned.1.call-update) | async-done | bytes 65552 | tf_op jit(solution)/shard_map/reduce_scatter | solution.py:351
  129.8 7.4 %all_gather.13 = bf16[128,1024]{1,0:T(8,128)(2,1)S(1)} all-gather(bf16[32,1024]{1,0:T(8,128)(2,1)S(1)} %multiply_convert_fusion.3), channel_id=1, replica_groups=mesh['ctx'=32,'tp'=4] {'tp'}, dimensions={0}, use_global_device_ids=true | all-gather | bytes 327680 | tf_op jit(solution)/shard_map/all_gather | solution.py:347
  137.2 2.3 fusion.87
  140.1 1.7 multiply_convert_fusion
  142.7 1.6 fusion.31
  148.2 1.6 copy.90
  153.7 17.0 %reduce-scatter.9.cloned.1.call-done = bf16[32,1024]{1,0:T(8,128)(2,1)} async-done(((bf16[128,1024]{1,0:T(8,128)(2,1)}), bf16[32,1024]{1,0:T(8,128)(2,1)}) %reduce-scatter.9.cloned.1.call-update) | async-done | bytes 65552 | tf_op jit(solution)/shard_map/reduce_scatter | solution.py:351
  170.7 1.5 fusion.51
  173.8 7.6 %all_gather.15 = bf16[128,1024]{1,0:T(8,128)(2,1)S(1)} all-gather(bf16[32,1024]{1,0:T(8,128)(2,1)S(1)} %fusion.77), channel_id=1, replica_groups=mesh['ctx'=32,'tp'=4] {'tp'}, dimensions={0}, use_global_device_ids=true | all-gather | bytes 327680 | tf_op jit(solution)/shard_map/all_gather | solution.py:347
  182.1 2.0 convolution_convert_fusion.9
  184.1 1.6 reshape.328
  185.7 1.7 copy.84
  188.6 4.9 fusion.16
  193.5 1.7 fusion.1
  195.3 1.5 fusion.17
  196.8 1.8 convolution_bitcast_fusion.2
  198.7 4.4 reshape.330
  203.1 4.4 reshape.331
  207.4 5.0 maximum_bitcast_fusion
  212.5 5.5 copy.93
  218.1 39.2 %shard_map.238 = f32[128,256]{1,0:T(8,128)} custom-call(bf16[4096,256]{1,0:T(8,128)(2,1)} %bitcast.191), custom_call_target="tpu_custom_call" | custom-call | tf_op jit(solution)/shard_map/pallas_call | solution.py:120
  259.5 1.9 copy.85
  263.9 1.7 copy.89
  265.6 1.7 copy.86
  271.2 1.9 fusion.28
  273.4 2.2 convolution_convert_fusion.7
  275.7 2.1 fusion.27
  278.0 1.8 fusion.30
  279.7 1.9 fusion.29
  281.6 2.0 fusion.26
  283.6 3.3 fusion.8
  286.9 2.3 fusion.7
  289.2 2.4 fusion.10.whole_ref
  291.6 11.6 %reduce-scatter.11.cloned.1.call-done = bf16[32,1024]{1,0:T(8,128)(2,1)} async-done(((bf16[128,1024]{1,0:T(8,128)(2,1)}), bf16[32,1024]{1,0:T(8,128)(2,1)}) %reduce-scatter.11.cloned.1.call-update) | async-done | bytes 65552 | tf_op jit(solution)/shard_map/reduce_scatter | solution.py:351
  304.3 15.5 %psum.7 = f32[2176]{0:T(1024)S(1)} all-reduce(f32[2176]{0:T(1024)S(1)} %concatenate.47), channel_id=1, replica_groups=mesh['ctx'=32,'tp'=4] {'tp'}, use_global_device_ids=true, to_apply=%region_23.24 | all-reduce | flops 2176 | bytes 17408 | tf_op jit(solution)/shard_map/psum | solution.py:533
  320.3 237.9 %shard_map.239 = (bf16[1024,4224]{1,0:T(8,128)(2,1)}, f32[8,384]{1,0:T(8,128)}) custom-call(bf16[1024,4224]{1,0:T(8,128)(2,1)} %fusion.10.whole_ref, f32[8,384]{1,0:T(8,128)} %reshape.333.extra_ref), custom_call_target="tpu_custom_call" | custom-call | tf_op jit(solution)/shard_map/pallas_call | solution.py:250
  558.3 10.5 %convert_element_type.165 = f32[1024,4224]{1,0:T(8,128)} convert(bf16[1024,4224]{1,0:T(8,128)(2,1)} %get-tuple-element.16) | non-fusion elementwise | flops 4325376 | bytes 25952256 | tf_op jit(solution)/shard_map/convert_element_type | solution.py:541
  568.8 5.2 slice_bitcast_fusion
  574.0 1.7 slice_bitcast_fusion.1
  575.7 4.3 fusion.80
  581.1 2.1 slice.109
  583.2 6.2 %copy.103 = f32[1152,1024]{1,0:T(8,128)} copy(f32[1152,1024]{0,1:T(8,128)} %slice_bitcast_fusion) | data formatting | bytes 9437184
  591.3 2.1 fusion.81
  593.4 1.8 fusion.46
  (183 shorter events, 44.0 us)
Async XLA Ops:
  7.2 132.9 %copy-start = (bf16[1152,1024]{1,0:T(8,128)(2,1)S(1)}, bf16[1152,1024]{1,0:T(8,128)(2,1)}, u32[]{:S(2)}) copy-start(bf16[1152,1024]{1,0:T(8,128)(2,1)} %param.26) | copy-start | bytes 7077892
  7.2 120.5 %reduce-scatter.5.cloned.1.call-start = ((), (), s32[]{:S(2)}) async-start(), calls=%async_computation.4 | async-start | bytes 327680 | tf_op jit(solution)/shard_map/reduce_scatter | solution.py:351
  9.3 0.9 copy-start.49
  17.5 51.4 %copy-start.5 = (bf16[128,1024]{1,0:T(8,128)(2,1)}, bf16[128,1024]{1,0:T(8,128)(2,1)S(1)}, u32[]{:S(2)}) copy-start(bf16[128,1024]{1,0:T(8,128)(2,1)S(1)} %all_gather.12) | copy-start | bytes 786436
  18.8 50.1 %copy-start.29 = (f32[128,128]{0,1:T(8,128)}, f32[128,128]{0,1:T(8,128)S(1)}, u32[]{:S(2)}) copy-start(f32[128,128]{0,1:T(8,128)S(1)} %get-tuple-element.96) | copy-start | bytes 196612
  18.9 5.3 copy-start.46
  23.4 45.5 %copy-start.35 = (f32[128,32]{0,1:T(8,128)}, f32[128,32]{0,1:T(8,128)S(1)}, u32[]{:S(2)}) copy-start(f32[128,32]{0,1:T(8,128)S(1)} %get-tuple-element.94) | copy-start | bytes 49156
  73.4 16.9 %copy-start.17 = (f32[128,256]{0,1:T(8,128)}, f32[128,256]{0,1:T(8,128)S(1)}, u32[]{:S(2)}) copy-start(f32[128,256]{0,1:T(8,128)S(1)} %copy.78) | copy-start | bytes 393220
  73.5 2.1 copy-start.42
  88.3 3.2 copy-start.14
  88.3 3.2 copy-start.31
  90.4 3.2 copy-start.3
  90.4 3.2 copy-start.41
  91.5 2.0 copy-start.44
  91.5 7.5 %copy-start.33 = (bf16[32,1024]{1,0:T(8,128)(2,1)S(1)}, bf16[32,1024]{1,0:T(8,128)(2,1)}, u32[]{:S(2)}) copy-start(bf16[32,1024]{1,0:T(8,128)(2,1)} %param.27) | copy-start | bytes 196612
  91.5 36.2 %copy-start.11 = (bf16[32,1024]{1,0:T(8,128)(2,1)S(1)}, bf16[32,1024]{1,0:T(8,128)(2,1)}, u32[]{:S(2)}) copy-start(bf16[32,1024]{1,0:T(8,128)(2,1)} %param.14) | copy-start | bytes 196612
  98.9 71.8 %reduce-scatter.9.cloned.1.call-start = ((), (), s32[]{:S(2)}) async-start(), calls=%async_computation.6 | async-start | bytes 327680 | tf_op jit(solution)/shard_map/reduce_scatter | solution.py:351
  127.7 11.8 %copy-start.8 = (bf16[1024,1152]{1,0:T(8,128)(2,1)S(1)}, bf16[1024,1152]{1,0:T(8,128)(2,1)}, u32[]{:S(2)}) copy-start(bf16[1024,1152]{1,0:T(8,128)(2,1)} %param.25) | copy-start | bytes 7077892
  127.7 12.3 %copy-start.27 = (bf16[128,1024]{1,0:T(8,128)(2,1)S(1)}, bf16[128,1024]{1,0:T(8,128)(2,1)}, u32[]{:S(2)}) copy-start(bf16[128,1024]{1,0:T(8,128)(2,1)} %all_gather.14) | copy-start | bytes 786436
  128.9 10.6 %copy-start.47 = (f32[32]{0:T(128)}, f32[32]{0:T(128)S(1)}, u32[]{:S(2)}) copy-start(f32[32]{0:T(128)S(1)} %add_rsqrt_fusion.2) | copy-start | bytes 388
  137.2 2.3 copy-start.9
  139.5 2.3 copy-start.7
  141.8 0.9 copy-start.20
  141.8 0.9 copy-start.23
  141.8 28.9 %copy-start.19 = (bf16[32,1024]{1,0:T(8,128)(2,1)S(1)}, bf16[32,1024]{1,0:T(8,128)(2,1)}, u32[]{:S(2)}) copy-start(bf16[32,1024]{1,0:T(8,128)(2,1)} %reduce-scatter.5.cloned.1.call-done) | copy-start | bytes 196612
  144.3 158.8 %reduce-scatter.11.cloned.1.call-start = ((), (), s32[]{:S(2)}) async-start(), calls=%async_computation.7 | async-start | bytes 327680 | tf_op jit(solution)/shard_map/reduce_scatter | solution.py:351
  172.2 0.6 copy-start.53
  181.4 0.7 copy-start.12
  187.4 6.1 %copy-start.4 = (f32[2,2,2048,64,2]{2,3,4,1,0:T(8,128)S(1)}, f32[2,2,2048,64,2]{2,3,4,1,0:T(8,128)}, u32[]{:S(2)}) copy-start(f32[2,2,2048,64,2]{2,3,4,1,0:T(8,128)} %copy-done.3) | copy-start | bytes 12582916
  187.4 6.1 %copy-start.15 = (pred[64,2048]{1,0:T(8,128)(4,1)S(1)}, pred[64,2048]{1,0:T(8,128)(4,1)}, u32[]{:S(2)}) copy-start(pred[64,2048]{1,0:T(8,128)(4,1)} %copy-done.14) | copy-start | bytes 393220
  187.4 6.1 %copy-start.32 = (bf16[2,2048,128]{1,2,0:T(8,128)(2,1)S(1)}, bf16[2,2048,128]{1,2,0:T(8,128)(2,1)}, u32[]{:S(2)}) copy-start(bf16[2,2048,128]{1,2,0:T(8,128)(2,1)} %copy.81) | copy-start | bytes 3145732
  187.4 6.1 %copy-start.34 = (bf16[2,64,2,2,64]{1,4,3,2,0:T(8,128)(2,1)S(1)}, bf16[2,64,2,2,64]{1,4,3,2,0:T(8,128)(2,1)}, u32[]{:S(2)}) copy-start(bf16[2,64,2,2,64]{1,4,3,2,0:T(8,128)(2,1)} %copy.84) | copy-start | bytes 196612
  187.4 6.1 %copy-start.51 = (f32[2,2,2,64]{3,2,1,0:T(2,128)S(1)}, f32[2,2,2,64]{3,2,1,0:T(2,128)}, u32[]{:S(2)}) copy-start(f32[2,2,2,64]{3,2,1,0:T(2,128)} %log_add_fusion) | copy-start | bytes 6148
  193.5 1.8 copy-start.25
  193.5 1.8 copy-start.26
  212.5 45.8 %copy-start.36 = (f32[128,32]{0,1:T(8,128)S(1)}, f32[128,32]{0,1:T(8,128)}, u32[]{:S(2)}) copy-start(f32[128,32]{0,1:T(8,128)} %copy-done.35) | copy-start | bytes 49156
  212.5 45.8 %copy-start.30 = (f32[128,128]{0,1:T(8,128)S(1)}, f32[128,128]{0,1:T(8,128)}, u32[]{:S(2)}) copy-start(f32[128,128]{0,1:T(8,128)} %copy-done.29) | copy-start | bytes 196612
  212.5 45.8 %copy-start.52 = (f32[64]{0:T(128)S(1)}, f32[64]{0:T(128)}, u32[]{:S(2)}) copy-start(f32[64]{0:T(128)} %param.21) | copy-start | bytes 772
  212.5 50.0 %copy-start.18 = (f32[128,256]{0,1:T(8,128)S(1)}, f32[128,256]{0,1:T(8,128)}, u32[]{:S(2)}) copy-start(f32[128,256]{0,1:T(8,128)} %copy-done.17) | copy-start | bytes 393220
  212.5 50.0 %copy-start.48 = (f32[64]{0:T(128)S(1)}, f32[64]{0:T(128)}, u32[]{:S(2)}) copy-start(f32[64]{0:T(128)} %param.20) | copy-start | bytes 772
  212.5 54.7 %copy-start.21 = (f32[128,256]{1,0:T(8,128)S(1)}, f32[128,256]{1,0:T(8,128)}, u32[]{:S(2)}) copy-start(f32[128,256]{1,0:T(8,128)} %fusion.86) | copy-start | bytes 393220
  218.1 50.3 %copy-start.16 = (bf16[1024,256]{1,0:T(8,128)(2,1)S(1)}, bf16[1024,256]{1,0:T(8,128)(2,1)}, u32[]{:S(2)}) copy-start(bf16[1024,256]{1,0:T(8,128)(2,1)} %param.17) | copy-start | bytes 1572868
  263.2 12.4 %copy-start.6 = (bf16[128,1024]{1,0:T(8,128)(2,1)S(1)}, bf16[128,1024]{1,0:T(8,128)(2,1)}, u32[]{:S(2)}) copy-start(bf16[128,1024]{1,0:T(8,128)(2,1)} %copy-done.5) | copy-start | bytes 786436
  268.3 0.6 copy-start.38
  268.9 12.7 %copy-start.13 = (bf16[128,1024]{1,0:T(8,128)(2,1)S(1)}, bf16[128,1024]{1,0:T(8,128)(2,1)}, u32[]{:S(2)}) copy-start(bf16[128,1024]{1,0:T(8,128)(2,1)} %copy-done.12) | copy-start | bytes 786436
  269.9 5.7 copy-start.37
  269.9 13.7 %copy-start.10 = (bf16[128,1024]{1,0:T(8,128)(2,1)S(1)}, bf16[128,1024]{1,0:T(8,128)(2,1)}, u32[]{:S(2)}) copy-start(bf16[128,1024]{1,0:T(8,128)(2,1)} %copy-done.9) | copy-start | bytes 786436
  273.2 320.3 %reduce-scatter.7.cloned.1.call-start = ((), (), s32[]{:S(2)}) async-start(), calls=%async_computation.5 | async-start | bytes 327680 | tf_op jit(solution)/shard_map/reduce_scatter | solution.py:351
  275.6 11.3 %copy-start.24 = (bf16[128,1152]{1,0:T(8,128)(2,1)S(1)}, bf16[128,1152]{1,0:T(8,128)(2,1)}, u32[]{:S(2)}) copy-start(bf16[128,1152]{1,0:T(8,128)(2,1)} %copy-done.23) | copy-start | bytes 884740
  275.6 13.6 %copy-start.22 = (bf16[128,1152]{1,0:T(8,128)(2,1)S(1)}, bf16[128,1152]{1,0:T(8,128)(2,1)}, u32[]{:S(2)}) copy-start(bf16[128,1152]{1,0:T(8,128)(2,1)} %get-tuple-element.70) | copy-start | bytes 884740
  275.7 13.5 %copy-start.28 = (bf16[128,1024]{1,0:T(8,128)(2,1)S(1)}, bf16[128,1024]{1,0:T(8,128)(2,1)}, u32[]{:S(2)}) copy-start(bf16[128,1024]{1,0:T(8,128)(2,1)} %all_gather.14) | copy-start | bytes 786436
  283.6 19.5 %copy-start.40 = (f32[1024]{0:T(1024)S(1)}, f32[1024]{0:T(1024)}, u32[]{:S(2)}) copy-start(f32[1024]{0:T(1024)} %param.16) | copy-start | bytes 12292
  283.6 19.5 %copy-start.50 = (f32[32]{0:T(128)S(1)}, f32[32]{0:T(128)}, u32[]{:S(2)}) copy-start(f32[32]{0:T(128)} %copy-done.49) | copy-start | bytes 388
  283.6 20.5 %copy-start.43 = (f32[1024]{0:T(1024)S(1)}, f32[1024]{0:T(1024)}, u32[]{:S(2)}) copy-start(f32[1024]{0:T(1024)} %get-tuple-element.56) | copy-start | bytes 12292
  568.8 6.9 %copy-start.2 = (bf16[1024,4224]{1,0:T(8,128)(2,1)S(1)}, bf16[1024,4224]{1,0:T(8,128)(2,1)}, u32[]{:S(2)}) copy-start(bf16[1024,4224]{1,0:T(8,128)(2,1)} %get-tuple-element.16) | copy-start | bytes 25952260
  575.7 4.4 copy-start.45
  583.2 11.9 %copy-start.1 = (bf16[1152,1024]{1,0:T(8,128)(2,1)S(1)}, bf16[1152,1024]{1,0:T(8,128)(2,1)}, u32[]{:S(2)}) copy-start(bf16[1152,1024]{1,0:T(8,128)(2,1)} %param.26) | copy-start | bytes 7077892
  589.4 4.0 copy-start.39
Sparse Core Ops, SparseCore 0:
  99.1 28.6 reduce-scatter.4
  144.4 26.2 reduce-scatter.8
  273.3 29.8 reduce-scatter.10
  305.7 63.8 reduce-scatter.6

commit v3 on v0

--- a/solution.py
+++ b/solution.py
@@ -21,11 +21,18 @@
     return order
 
 
-def _enter(n, me, peer_axis):
+def _place(axis, peer, other):
+    return (peer, other) if axis == "ctx" else (other, peer)
+
+
+def _enter(n, me, peer_axis, axis="ctx"):
     barrier = pltpu.get_barrier_semaphore()
     for k in _shifts(n):
         pl.semaphore_signal(
-            barrier, 1, device_id=(lax.rem(me + k, n), peer_axis), device_id_type=MESH
+            barrier,
+            1,
+            device_id=_place(axis, lax.rem(me + k, n), peer_axis),
+            device_id_type=MESH,
         )
     pl.semaphore_wait(barrier, n - 1)
 
@@ -76,7 +83,7 @@
     )(part)
 
 
-def _scatter_sum(n, me, other, whole_ref, held, send_sem, recv_sem, rows):
+def _scatter_sum(n, me, other, whole_ref, held, send_sem, recv_sem, rows, axis="ctx"):
     copies = []
     for k in _shifts(n):
         target = lax.rem(me + k, n)
@@ -85,7 +92,7 @@
             dst_ref=held.at[k],
             send_sem=send_sem.at[k],
             recv_sem=recv_sem.at[k],
-            device_id=(target, other),
+            device_id=_place(axis, target, other),
             device_id_type=MESH,
         )
         copy.start()
@@ -98,7 +105,7 @@
             dst_ref=held.at[k],
             send_sem=send_sem.at[k],
             recv_sem=recv_sem.at[k],
-            device_id=(source, other),
+            device_id=_place(axis, source, other),
             device_id_type=MESH,
         ).wait_recv()
         total = total + held[k].astype(jnp.float32)
@@ -107,18 +114,18 @@
     return total
 
 
-def _scatter_kernel(n, whole_ref, out_ref, held, send_sem, recv_sem):
-    me = lax.axis_index("ctx")
-    other = lax.axis_index("tp")
+def _scatter_kernel(n, axis, whole_ref, out_ref, held, send_sem, recv_sem):
+    me = lax.axis_index(axis)
+    other = lax.axis_index("tp" if axis == "ctx" else "ctx")
     rows = out_ref.shape[0]
-    _enter(n, me, other)
-    out_ref[...] = _scatter_sum(n, me, other, whole_ref, held, send_sem, recv_sem, rows)
-
-
-def ctx_scatter(whole, n, collective_id):
+    _enter(n, me, other, axis)
+    out_ref[...] = _scatter_sum(n, me, other, whole_ref, held, send_sem, recv_sem, rows, axis)
+
+
+def ctx_scatter(whole, n, collective_id, axis="ctx"):
     rows, cols = whole.shape[0] // n, whole.shape[1]
     return pl.pallas_call(
-        functools.partial(_scatter_kernel, n),
+        functools.partial(_scatter_kernel, n, axis),
         out_shape=jax.ShapeDtypeStruct((rows, cols), jnp.float32),
         in_specs=[pl.BlockSpec(memory_space=pltpu.VMEM)],
         out_specs=pl.BlockSpec(memory_space=pltpu.VMEM),
@@ -347,10 +354,10 @@
     return lax.all_gather(rows_low, "tp", axis=0, tiled=True)
 
 
-def reduce_rows(partial_rows):
-    return lax.psum_scatter(
-        partial_rows.astype(jnp.bfloat16), "tp", scatter_dimension=0, tiled=True
-    ).astype(jnp.float32)
+def reduce_rows(partial_rows, collective_id):
+    return ctx_scatter(
+        partial_rows.astype(jnp.bfloat16), lax.axis_size("tp"), collective_id, "tp"
+    )
 
 
 def per_device(
@@ -432,7 +439,8 @@
     attn_rows = jnp.transpose(weighted / weight_total[..., None], (0, 3, 1, 2, 4))
     attn_low = attn_rows.reshape(rows_total, query_heads * head_dim).astype(jnp.bfloat16)
     residual_mid = residual_in + reduce_rows(
-        jnp.dot(attn_low, output_weight, preferred_element_type=jnp.float32)
+        jnp.dot(attn_low, output_weight, preferred_element_type=jnp.float32),
+        3
     )
     normed_two, inverse_two = rms_forward(residual_mid, ffn_gain)
     rows_two = gather_rows(normed_two.astype(jnp.bfloat16))
@@ -441,7 +449,8 @@
     gate_sig = jax.nn.sigmoid(gate_pre)
     activated = (gate_pre * gate_sig * up_pre).astype(jnp.bfloat16)
     block_output = residual_mid + reduce_rows(
-        jnp.dot(activated, down_weight, preferred_element_type=jnp.float32)
+        jnp.dot(activated, down_weight, preferred_element_type=jnp.float32),
+        4
     )
     grad_rows = gather_rows(cotangent)
     grad_down_t = jnp.dot(grad_rows.T, activated, preferred_element_type=jnp.float32)
@@ -454,7 +463,8 @@
     grad_up = jnp.dot(rows_two.T, grad_up_pre, preferred_element_type=jnp.float32)
     grad_normed_two = reduce_rows(
         jnp.dot(grad_gate_pre, gate_weight.T, preferred_element_type=jnp.float32)
-        + jnp.dot(grad_up_pre, up_weight.T, preferred_element_type=jnp.float32)
+        + jnp.dot(grad_up_pre, up_weight.T, preferred_element_type=jnp.float32),
+        5
     )
     through_two, ffn_terms = rms_backward(residual_mid, inverse_two, ffn_gain, grad_normed_two)
     grad_mid = cotangent.astype(jnp.float32) + through_two
@@ -517,7 +527,8 @@
     grad_normed_one = reduce_rows(
         jnp.dot(grad_query_low, query_weight.T, preferred_element_type=jnp.float32)
         + jnp.dot(grad_key_low, key_weight.T, preferred_element_type=jnp.float32)
-        + jnp.dot(grad_value_low, value_weight.T, preferred_element_type=jnp.float32)
+        + jnp.dot(grad_value_low, value_weight.T, preferred_element_type=jnp.float32),
+        6
     )
     through_one, attn_terms = rms_backward(residual_in, inverse_one, attn_gain, grad_normed_one)
     input_grad = grad_mid + through_one

time: 588 us -> 576 us (0.980)
  the two profiles are of different devices: /device:TPU:28 before, /device:TPU:20 now
where the time goes in v3:
time: 576 us; the launch traced here: 574 us
  Pallas kernels  346 us (60%)
  local copies, waits for them, and re-layouts  80.2 us (14%)
  matrix products  55.1 us (10%)
  blocking collectives  45.6 us (8%)
  other arithmetic  44.7 us (8%)
    pallas_call x1, Pallas kernels, ctx_sum(): pl.pallas_call(functools.partial(_sum_kernel, n, spans), out_shape=(jax.S...  229 us
    pallas_call x5, Pallas kernels, ctx_scatter(): pl.pallas_call(functools.partial(_scatter_kernel, n, axis), out_shape=jax...  77.3 us
    pallas_call x1, Pallas kernels, ctx_gather(): pl.pallas_call(functools.partial(_gather_kernel, n), out_shape=jax.ShapeD...  40 us
    all_gather x4, blocking collectives, gather_rows(): return lax.all_gather(rows_low, 'tp', axis=0, tiled=True)  30.5 us
    psum x1, blocking collectives, per_device(): gain_flat = lax.psum(jnp.concatenate(gain_parts), 'tp')  15.1 us
    unnamed x108, local copies, waits for them, and re-layouts  12.8 us

profile of v3, /device:TPU:20, one launch (start us, length us, event | category | flops | bytes accessed | tf_op | source)
XLA Modules:
  0.0 573.8 jit_solution(5191621800805736498)
XLA Ops:
  2.7 8.1 %all_gather.12 = bf16[128,1024]{1,0:T(8,128)(2,1)S(1)} all-gather(bf16[32,1024]{1,0:T(8,128)(2,1)S(1)} %fusion.40), channel_id=1, replica_groups=mesh['ctx'=32,'tp'=4] {'tp'}, dimensions={0}, use_global_device_ids=true | all-gather | bytes 327680 | tf_op jit(solution)/shard_map/all_gather | solution.py:354
  18.8 40.0 %shard_map.237 = bf16[4096,256]{1,0:T(8,128)(2,1)} custom-call(bf16[128,256]{1,0:T(8,128)(2,1)} %pad_maximum_fusion.2.part_ref), custom_call_target="tpu_custom_call" | custom-call | tf_op jit(solution)/shard_map/pallas_call | solution.py:74
  58.8 1.7 copy.76
  60.5 1.7 fusion.75
  62.2 1.5 copy.77
  63.7 2.0 fusion.79
  67.5 1.4 subtract_convert_fusion
  68.9 1.5 concatenate.38
  70.4 1.6 copy.79
  72.0 1.5 concatenate.39
  73.5 1.6 copy.80
  76.6 1.4 add.160
  78.8 2.0 fusion.2
  80.8 2.0 copy-done.1
  84.6 2.3 copy.81
  86.8 4.5 fusion.78
  91.3 1.7 copy.82
  94.0 2.0 convolution_convert_fusion.8.whole_ref
  96.1 9.2 %shard_map.238 = f32[32,1024]{1,0:T(8,128)} custom-call(bf16[128,1024]{1,0:T(8,128)(2,1)} %convolution_convert_fusion.8.whole_ref), custom_call_target="tpu_custom_call" | custom-call | tf_op jit(solution)/shard_map/pallas_call | solution.py:127
  107.3 7.4 %all_gather.13 = bf16[128,1024]{1,0:T(8,128)(2,1)S(1)} all-gather(bf16[32,1024]{1,0:T(8,128)(2,1)S(1)} %multiply_convert_fusion.3), channel_id=1, replica_groups=mesh['ctx'=32,'tp'=4] {'tp'}, dimensions={0}, use_global_device_ids=true | all-gather | bytes 327680 | tf_op jit(solution)/shard_map/all_gather | solution.py:354
  114.7 2.3 fusion.80
  117.5 7.5 %all_gather.14 = bf16[128,1024]{1,0:T(8,128)(2,1)S(1)} all-gather(bf16[32,1024]{1,0:T(8,128)(2,1)S(1)} %copy-done.29), channel_id=1, replica_groups=mesh['ctx'=32,'tp'=4] {'tp'}, dimensions={0}, use_global_device_ids=true | all-gather | bytes 327680 | tf_op jit(solution)/shard_map/all_gather | solution.py:354
  125.0 1.7 multiply_convert_fusion
  127.7 1.6 fusion.31.whole_ref
  129.3 9.0 %shard_map.240 = f32[32,1024]{1,0:T(8,128)} custom-call(bf16[128,1024]{1,0:T(8,128)(2,1)} %fusion.31.whole_ref), custom_call_target="tpu_custom_call" | custom-call | tf_op jit(solution)/shard_map/pallas_call | solution.py:127
  138.3 1.6 multiply_reduce_fusion.1
  140.9 7.5 %all_gather.15 = bf16[128,1024]{1,0:T(8,128)(2,1)S(1)} all-gather(bf16[32,1024]{1,0:T(8,128)(2,1)S(1)} %fusion.70), channel_id=1, replica_groups=mesh['ctx'=32,'tp'=4] {'tp'}, dimensions={0}, use_global_device_ids=true | all-gather | bytes 327680 | tf_op jit(solution)/shard_map/all_gather | solution.py:354
  150.0 1.6 reshape.328
  151.6 1.7 copy.84
  154.3 4.4 fusion.1
  160.0 1.5 fusion.17
  161.6 4.4 reshape.330
  166.0 4.3 fusion.16
  170.3 4.4 reshape.331
  174.7 5.0 maximum_bitcast_fusion
  179.7 5.4 copy.93
  185.2 41.1 %shard_map.241 = f32[128,256]{1,0:T(8,128)} custom-call(bf16[4096,256]{1,0:T(8,128)(2,1)} %bitcast.191), custom_call_target="tpu_custom_call" | custom-call | tf_op jit(solution)/shard_map/pallas_call | solution.py:127
  226.3 1.5 slice.82
  227.8 1.6 copy.94
  230.2 1.5 multiply_reduce_fusion.7
  234.7 2.1 fusion.56
  236.8 2.7 convolution_bitcast_fusion.2
  240.8 1.6 pad_maximum_fusion.1
  243.2 1.7 copy.86
  246.2 1.7 copy.90
  253.0 1.9 fusion.28.whole_ref
  254.9 9.0 %shard_map.242 = f32[32,1024]{1,0:T(8,128)} custom-call(bf16[128,1024]{1,0:T(8,128)(2,1)} %fusion.28.whole_ref), custom_call_target="tpu_custom_call" | custom-call | tf_op jit(solution)/shard_map/pallas_call | solution.py:127
  265.3 15.1 %psum.7 = f32[2176]{0:T(1024)S(1)} all-reduce(f32[2176]{0:T(1024)S(1)} %concatenate.47), channel_id=1, replica_groups=mesh['ctx'=32,'tp'=4] {'tp'}, use_global_device_ids=true, to_apply=%region_19.20 | all-reduce | flops 2176 | bytes 17408 | tf_op jit(solution)/shard_map/psum | solution.py:544
  281.1 2.1 fusion.27
  283.2 1.8 fusion.30
  284.9 1.9 fusion.29
  286.8 2.0 fusion.26
  288.8 3.2 fusion.8
  292.1 2.3 fusion.7
  294.4 2.4 fusion.10.whole_ref
  296.7 228.8 %shard_map.243 = (bf16[1024,4224]{1,0:T(8,128)(2,1)}, f32[8,384]{1,0:T(8,128)}) custom-call(bf16[1024,4224]{1,0:T(8,128)(2,1)} %fusion.10.whole_ref, f32[8,384]{1,0:T(8,128)} %reshape.333.extra_ref), custom_call_target="tpu_custom_call" | custom-call | tf_op jit(solution)/shard_map/pallas_call | solution.py:257
  525.6 10.5 %convert_element_type.149 = f32[1024,4224]{1,0:T(8,128)} convert(bf16[1024,4224]{1,0:T(8,128)(2,1)} %get-tuple-element.16) | non-fusion elementwise | flops 4325376 | bytes 25952256 | tf_op jit(solution)/shard_map/convert_element_type | solution.py:552
  536.1 4.8 slice_bitcast_fusion
  540.9 6.0 %copy.103 = f32[1152,1024]{1,0:T(8,128)} copy(f32[1152,1024]{0,1:T(8,128)} %slice_bitcast_fusion) | data formatting | bytes 9437184
  549.5 6.7 %fusion.73 = (f32[1024,1152]{1,0:T(8,128)}, f32[1024,1152]{1,0:T(8,128)}) fusion(bf16[1024,4224]{1,0:T(8,128)(2,1)} %get-tuple-element.16), kind=kLoop, calls=%fused_computation.168 | loop fusion | bytes 18874368 | tf_op jit(solution)/shard_map/slice | solution.py:556
  556.4 2.2 fusion.74
  558.5 2.1 slice.109
  563.0 9.0 %shard_map.239 = f32[32,1024]{1,0:T(8,128)} custom-call(bf16[128,1024]{1,0:T(8,128)(2,1)} %convolution_convert_fusion.7.whole_ref), custom_call_target="tpu_custom_call" | custom-call | tf_op jit(solution)/shard_map/pallas_call | solution.py:127
  572.1 1.7 fusion.44
  (173 shorter events, 43.8 us)
Async XLA Ops:
  0.6 124.4 %copy-start = (bf16[1152,1024]{1,0:T(8,128)(2,1)S(1)}, bf16[1152,1024]{1,0:T(8,128)(2,1)}, u32[]{:S(2)}) copy-start(bf16[1152,1024]{1,0:T(8,128)(2,1)} %param.26) | copy-start | bytes 7077892
  1.8 0.9 copy-start.47
  10.9 51.4 %copy-start.2 = (bf16[128,1024]{1,0:T(8,128)(2,1)}, bf16[128,1024]{1,0:T(8,128)(2,1)S(1)}, u32[]{:S(2)}) copy-start(bf16[128,1024]{1,0:T(8,128)(2,1)S(1)} %all_gather.12) | copy-start | bytes 786436
  12.2 0.6 copy-start.27
  12.8 3.8 copy-start.44
  16.8 45.4 %copy-start.32 = (f32[128,32]{0,1:T(8,128)}, f32[128,32]{0,1:T(8,128)S(1)}, u32[]{:S(2)}) copy-start(f32[128,32]{0,1:T(8,128)S(1)} %get-tuple-element.96) | copy-start | bytes 49156
  66.7 9.8 %copy-start.13 = (f32[128,256]{0,1:T(8,128)}, f32[128,256]{0,1:T(8,128)S(1)}, u32[]{:S(2)}) copy-start(f32[128,256]{0,1:T(8,128)S(1)} %copy.78) | copy-start | bytes 393220
  66.8 2.1 copy-start.40
  78.8 8.0 %copy-start.12 = (pred[64,2048]{1,0:T(8,128)(4,1)}, pred[64,2048]{1,0:T(8,128)(4,1)S(1)}, u32[]{:S(2)}) copy-start(pred[64,2048]{1,0:T(8,128)(4,1)S(1)} %broadcast_compare_fusion) | copy-start | bytes 393220
  80.8 2.0 copy-start.1
  80.8 3.1 copy-start.39
  83.9 0.6 copy-start.42
  94.0 2.0 copy-start.31
  94.0 23.5 %copy-start.29 = (bf16[32,1024]{1,0:T(8,128)(2,1)S(1)}, bf16[32,1024]{1,0:T(8,128)(2,1)}, u32[]{:S(2)}) copy-start(bf16[32,1024]{1,0:T(8,128)(2,1)} %param.27) | copy-start | bytes 196612
  105.3 11.7 %copy-start.5 = (bf16[1024,1152]{1,0:T(8,128)(2,1)S(1)}, bf16[1024,1152]{1,0:T(8,128)(2,1)}, u32[]{:S(2)}) copy-start(bf16[1024,1152]{1,0:T(8,128)(2,1)} %param.25) | copy-start | bytes 7077892
  106.5 33.4 %copy-start.45 = (f32[32]{0:T(128)}, f32[32]{0:T(128)S(1)}, u32[]{:S(2)}) copy-start(f32[32]{0:T(128)S(1)} %add_rsqrt_fusion.2) | copy-start | bytes 388
  114.7 2.3 copy-start.7
  117.0 9.8 %copy-start.4 = (bf16[1024,1152]{1,0:T(8,128)(2,1)S(1)}, bf16[1024,1152]{1,0:T(8,128)(2,1)}, u32[]{:S(2)}) copy-start(bf16[1024,1152]{1,0:T(8,128)(2,1)} %param.24) | copy-start | bytes 7077892
  125.0 2.6 copy-start.25
  126.7 0.9 copy-start.17
  126.7 0.9 copy-start.21
  126.7 11.5 %copy-start.35 = (f32[1024]{0:T(1024)S(1)}, f32[1024]{0:T(1024)}, u32[]{:S(2)}) copy-start(f32[1024]{0:T(1024)} %param.23) | copy-start | bytes 12292
  126.7 22.3 %copy-start.14 = (bf16[256,1024]{1,0:T(8,128)(2,1)S(1)}, bf16[256,1024]{1,0:T(8,128)(2,1)}, u32[]{:S(2)}) copy-start(bf16[256,1024]{1,0:T(8,128)(2,1)} %param.22) | copy-start | bytes 1572868
  139.9 8.5 %copy-start.50 = (f32[32]{0:T(128)}, f32[32]{0:T(128)S(1)}, u32[]{:S(2)}) copy-start(f32[32]{0:T(128)S(1)} %broadcast_multiply_fusion.3) | copy-start | bytes 388
  148.4 0.7 copy-start.9
  154.3 5.7 copy-start.23
  154.3 5.7 copy-start.24
  158.7 1.3 copy-start.6
  239.5 12.2 %copy-start.33 = (bf16[128,128]{0,1:T(8,128)(2,1)S(1)}, bf16[128,128]{0,1:T(8,128)(2,1)}, u32[]{:S(2)}) copy-start(bf16[128,128]{0,1:T(8,128)(2,1)} %get-tuple-element.80) | copy-start | bytes 98308
  239.6 13.4 %copy-start.28 = (f32[128,256]{1,0:T(8,128)S(1)}, f32[128,256]{1,0:T(8,128)}, u32[]{:S(2)}) copy-start(f32[128,256]{1,0:T(8,128)} %shard_map.241) | copy-start | bytes 393220
  239.6 24.3 %copy-start.15 = (bf16[32,1024]{1,0:T(8,128)(2,1)S(1)}, bf16[32,1024]{1,0:T(8,128)(2,1)}, u32[]{:S(2)}) copy-start(bf16[32,1024]{1,0:T(8,128)(2,1)} %param.14) | copy-start | bytes 196612
  239.6 24.3 %copy-start.37 = (f32[1024]{0:T(1024)S(1)}, f32[1024]{0:T(1024)}, u32[]{:S(2)}) copy-start(f32[1024]{0:T(1024)} %param.16) | copy-start | bytes 12292
  239.6 24.3 %copy-start.48 = (f32[32]{0:T(128)S(1)}, f32[32]{0:T(128)}, u32[]{:S(2)}) copy-start(f32[32]{0:T(128)} %copy-done.47) | copy-start | bytes 388
  239.6 25.4 %copy-start.52 = (f32[128]{0:T(128)S(1)}, f32[128]{0:T(128)}, u32[]{:S(2)}) copy-start(f32[128]{0:T(128)} %get-tuple-element.79) | copy-start | bytes 1540
  239.6 25.6 %copy-start.41 = (f32[1024]{0:T(1024)S(1)}, f32[1024]{0:T(1024)}, u32[]{:S(2)}) copy-start(f32[1024]{0:T(1024)} %get-tuple-element.56) | copy-start | bytes 12292
  239.6 41.4 %copy-start.3 = (bf16[128,1024]{1,0:T(8,128)(2,1)S(1)}, bf16[128,1024]{1,0:T(8,128)(2,1)}, u32[]{:S(2)}) copy-start(bf16[128,1024]{1,0:T(8,128)(2,1)} %copy-done.2) | copy-start | bytes 786436
  240.8 46.0 %copy-start.10 = (bf16[128,1024]{1,0:T(8,128)(2,1)S(1)}, bf16[128,1024]{1,0:T(8,128)(2,1)}, u32[]{:S(2)}) copy-start(bf16[128,1024]{1,0:T(8,128)(2,1)} %copy-done.9) | copy-start | bytes 786436
  243.2 45.6 %copy-start.8 = (bf16[128,1024]{1,0:T(8,128)(2,1)S(1)}, bf16[128,1024]{1,0:T(8,128)(2,1)}, u32[]{:S(2)}) copy-start(bf16[128,1024]{1,0:T(8,128)(2,1)} %copy-done.7) | copy-start | bytes 786436
  249.8 0.6 copy-start.34
  281.0 11.0 %copy-start.22 = (bf16[128,1152]{1,0:T(8,128)(2,1)S(1)}, bf16[128,1152]{1,0:T(8,128)(2,1)}, u32[]{:S(2)}) copy-start(bf16[128,1152]{1,0:T(8,128)(2,1)} %copy-done.21) | copy-start | bytes 884740
  281.0 13.3 %copy-start.19 = (bf16[128,1152]{1,0:T(8,128)(2,1)S(1)}, bf16[128,1152]{1,0:T(8,128)(2,1)}, u32[]{:S(2)}) copy-start(bf16[128,1152]{1,0:T(8,128)(2,1)} %get-tuple-element.72) | copy-start | bytes 884740
  281.0 13.3 %copy-start.26 = (bf16[128,1024]{1,0:T(8,128)(2,1)S(1)}, bf16[128,1024]{1,0:T(8,128)(2,1)}, u32[]{:S(2)}) copy-start(bf16[128,1024]{1,0:T(8,128)(2,1)} %copy-done.25) | copy-start | bytes 786436
  556.3 4.3 copy-start.43
  556.3 5.5 copy-start.20
  556.3 15.7 %copy-start.11 = (f32[32,1024]{1,0:T(8,128)S(1)}, f32[32,1024]{1,0:T(8,128)}, u32[]{:S(2)}) copy-start(f32[32,1024]{1,0:T(8,128)} %shard_map.240) | copy-start | bytes 393220
  556.3 15.7 %copy-start.16 = (bf16[32,1024]{1,0:T(8,128)(2,1)S(1)}, bf16[32,1024]{1,0:T(8,128)(2,1)}, u32[]{:S(2)}) copy-start(bf16[32,1024]{1,0:T(8,128)(2,1)} %param.14) | copy-start | bytes 196612
  556.3 15.8 %copy-start.18 = (f32[32,1024]{1,0:T(8,128)S(1)}, f32[32,1024]{1,0:T(8,128)}, u32[]{:S(2)}) copy-start(f32[32,1024]{1,0:T(8,128)} %shard_map.242) | copy-start | bytes 393220
  556.3 15.8 %copy-start.30 = (bf16[32,1024]{1,0:T(8,128)(2,1)S(1)}, bf16[32,1024]{1,0:T(8,128)(2,1)}, u32[]{:S(2)}) copy-start(bf16[32,1024]{1,0:T(8,128)(2,1)} %param.27) | copy-start | bytes 196612
  556.3 15.7 %copy-start.36 = (f32[1024]{0:T(1024)S(1)}, f32[1024]{0:T(1024)}, u32[]{:S(2)}) copy-start(f32[1024]{0:T(1024)} %param.23) | copy-start | bytes 12292
  556.3 15.7 %copy-start.38 = (f32[1024]{0:T(1024)S(1)}, f32[1024]{0:T(1024)}, u32[]{:S(2)}) copy-start(f32[1024]{0:T(1024)} %param.16) | copy-start | bytes 12292
  556.3 15.7 %copy-start.46 = (f32[32]{0:T(128)S(1)}, f32[32]{0:T(128)}, u32[]{:S(2)}) copy-start(f32[32]{0:T(128)} %copy-done.45) | copy-start | bytes 388
  556.3 15.7 %copy-start.49 = (f32[32]{0:T(128)S(1)}, f32[32]{0:T(128)}, u32[]{:S(2)}) copy-start(f32[32]{0:T(128)} %copy-done.47) | copy-start | bytes 388
  556.4 15.7 %copy-start.51 = (f32[32]{0:T(128)S(1)}, f32[32]{0:T(128)}, u32[]{:S(2)}) copy-start(f32[32]{0:T(128)} %copy-done.50) | copy-start | bytes 388

commit v4 on v3

--- a/solution.py
+++ b/solution.py
@@ -541,8 +541,15 @@
         jnp.sum(ffn_terms, axis=0),
     )
     gain_sizes = [part.shape[0] for part in gain_parts]
-    gain_flat = lax.psum(jnp.concatenate(gain_parts), "tp")
-    gain_pad = -gain_flat.shape[0] % 1024
+    gain_local = jnp.concatenate(gain_parts)
+    gain_pad = -gain_local.shape[0] % 1024
+    tp_count = lax.axis_size("tp")
+    gain_flat = ctx_scatter(
+        jnp.tile(jnp.pad(gain_local, (0, gain_pad)).reshape(8, -1), (tp_count, 1)),
+        tp_count,
+        7,
+        "tp",
+    ).reshape(-1)[: gain_local.shape[0]]
     summed, gains = ctx_sum(
         jnp.concatenate([part.astype(jnp.bfloat16) for part in weight_parts], axis=1),
         jnp.pad(gain_flat, (0, gain_pad)).reshape(8, -1),

time: 576 us -> 570 us (0.990)
  the two profiles are of different devices: /device:TPU:20 before, /device:TPU:28 now
where the time goes in v4:
time: 570 us; the launch traced here: 564 us
  Pallas kernels  351 us (62%)
  local copies, waits for them, and re-layouts  79.3 us (14%)
  matrix products  55.1 us (10%)
  other arithmetic  45.4 us (8%)
  blocking collectives  30.5 us (5%)
    pallas_call x1, Pallas kernels, ctx_sum(): pl.pallas_call(functools.partial(_sum_kernel, n, spans), out_shape=(jax.S...  224 us
    pallas_call x6, Pallas kernels, ctx_scatter(): pl.pallas_call(functools.partial(_scatter_kernel, n, axis), out_shape=jax...  85 us
    pallas_call x1, Pallas kernels, ctx_gather(): pl.pallas_call(functools.partial(_gather_kernel, n), out_shape=jax.ShapeD...  42 us
    all_gather x4, blocking collectives, gather_rows(): return lax.all_gather(rows_low, 'tp', axis=0, tiled=True)  30.5 us
    unnamed x110, local copies, waits for them, and re-layouts  12.8 us

profile of v4, /device:TPU:28, one launch (start us, length us, event | category | flops | bytes accessed | tf_op | source)
XLA Modules:
  0.0 563.7 jit_solution(222551102590277223)
XLA Ops:
  2.7 8.1 %all_gather.12 = bf16[128,1024]{1,0:T(8,128)(2,1)S(1)} all-gather(bf16[32,1024]{1,0:T(8,128)(2,1)S(1)} %fusion.40), channel_id=1, replica_groups=mesh['ctx'=32,'tp'=4] {'tp'}, dimensions={0}, use_global_device_ids=true | all-gather | bytes 327680 | tf_op jit(solution)/shard_map/all_gather | solution.py:354
  18.8 42.0 %shard_map.237 = bf16[4096,256]{1,0:T(8,128)(2,1)} custom-call(bf16[128,256]{1,0:T(8,128)(2,1)} %pad_maximum_fusion.2.part_ref), custom_call_target="tpu_custom_call" | custom-call | tf_op jit(solution)/shard_map/pallas_call | solution.py:74
  60.9 1.7 copy.76
  62.6 1.7 fusion.75
  64.3 1.5 copy.77
  65.8 2.0 fusion.79
  69.6 1.4 subtract_convert_fusion
  70.9 1.5 concatenate.38
  72.4 1.6 copy.79
  74.0 1.5 concatenate.39
  75.5 1.6 copy.80
  78.6 1.4 add.158
  80.9 2.0 fusion.2
  82.9 2.0 copy-done.1
  86.6 2.3 copy.81
  88.9 4.4 fusion.78
  93.3 1.7 copy.82
  96.1 2.0 convolution_convert_fusion.8.whole_ref
  98.1 9.2 %shard_map.238 = f32[32,1024]{1,0:T(8,128)} custom-call(bf16[128,1024]{1,0:T(8,128)(2,1)} %convolution_convert_fusion.8.whole_ref), custom_call_target="tpu_custom_call" | custom-call | tf_op jit(solution)/shard_map/pallas_call | solution.py:127
  109.3 7.4 %all_gather.13 = bf16[128,1024]{1,0:T(8,128)(2,1)S(1)} all-gather(bf16[32,1024]{1,0:T(8,128)(2,1)S(1)} %multiply_convert_fusion.3), channel_id=1, replica_groups=mesh['ctx'=32,'tp'=4] {'tp'}, dimensions={0}, use_global_device_ids=true | all-gather | bytes 327680 | tf_op jit(solution)/shard_map/all_gather | solution.py:354
  116.7 2.3 fusion.80
  119.6 7.5 %all_gather.14 = bf16[128,1024]{1,0:T(8,128)(2,1)S(1)} all-gather(bf16[32,1024]{1,0:T(8,128)(2,1)S(1)} %copy-done.29), channel_id=1, replica_groups=mesh['ctx'=32,'tp'=4] {'tp'}, dimensions={0}, use_global_device_ids=true | all-gather | bytes 327680 | tf_op jit(solution)/shard_map/all_gather | solution.py:354
  127.1 1.7 multiply_convert_fusion
  129.7 1.6 fusion.31.whole_ref
  131.3 9.0 %shard_map.240 = f32[32,1024]{1,0:T(8,128)} custom-call(bf16[128,1024]{1,0:T(8,128)(2,1)} %fusion.31.whole_ref), custom_call_target="tpu_custom_call" | custom-call | tf_op jit(solution)/shard_map/pallas_call | solution.py:127
  140.3 1.6 multiply_reduce_fusion.1
  142.9 7.5 %all_gather.15 = bf16[128,1024]{1,0:T(8,128)(2,1)S(1)} all-gather(bf16[32,1024]{1,0:T(8,128)(2,1)S(1)} %fusion.70), channel_id=1, replica_groups=mesh['ctx'=32,'tp'=4] {'tp'}, dimensions={0}, use_global_device_ids=true | all-gather | bytes 327680 | tf_op jit(solution)/shard_map/all_gather | solution.py:354
  152.0 1.6 reshape.334
  153.7 1.7 copy.84
  156.4 4.4 fusion.1
  162.1 1.5 fusion.17
  163.6 4.4 reshape.336
  168.0 4.3 fusion.16
  172.4 4.4 reshape.337
  176.8 5.0 maximum_bitcast_fusion
  181.8 5.4 copy.93
  187.2 41.0 %shard_map.241 = f32[128,256]{1,0:T(8,128)} custom-call(bf16[4096,256]{1,0:T(8,128)(2,1)} %bitcast.193), custom_call_target="tpu_custom_call" | custom-call | tf_op jit(solution)/shard_map/pallas_call | solution.py:127
  228.3 1.5 slice.85
  229.8 1.6 copy.94
  232.1 1.5 multiply_reduce_fusion.7
  236.7 2.1 fusion.56
  238.8 2.7 convolution_bitcast_fusion.2
  245.3 1.4 mul.494
  246.7 1.7 copy.90
  250.9 1.3 fusion.83
  253.5 1.9 fusion.28.whole_ref
  255.4 9.1 %shard_map.242 = f32[32,1024]{1,0:T(8,128)} custom-call(bf16[128,1024]{1,0:T(8,128)(2,1)} %fusion.28.whole_ref), custom_call_target="tpu_custom_call" | custom-call | tf_op jit(solution)/shard_map/pallas_call | solution.py:127
  266.5 6.8 %shard_map.243 = f32[8,384]{1,0:T(8,128)} custom-call(f32[32,384]{1,0:T(8,128)} %broadcast_bitcast_fusion.whole_ref), custom_call_target="tpu_custom_call" | custom-call | tf_op jit(solution)/shard_map/pallas_call | solution.py:127
  274.7 2.1 fusion.27
  276.8 1.7 fusion.30
  278.5 1.8 fusion.29
  280.4 2.0 fusion.26
  282.4 3.3 fusion.8
  285.7 2.3 fusion.7
  288.0 2.4 fusion.10.whole_ref
  290.4 224.3 %shard_map.244 = (bf16[1024,4224]{1,0:T(8,128)(2,1)}, f32[8,384]{1,0:T(8,128)}) custom-call(bf16[1024,4224]{1,0:T(8,128)(2,1)} %fusion.10.whole_ref, f32[8,384]{1,0:T(8,128)} %broadcast_select_fusion.extra_ref), custom_call_target="tpu_custom_call" | custom-call | tf_op jit(solution)/shard_map/pallas_call | solution.py:257
  514.7 10.5 %convert_element_type.150 = f32[1024,4224]{1,0:T(8,128)} convert(bf16[1024,4224]{1,0:T(8,128)(2,1)} %get-tuple-element.16) | non-fusion elementwise | flops 4325376 | bytes 25952256 | tf_op jit(solution)/shard_map/convert_element_type | solution.py:559
  525.2 4.8 slice_bitcast_fusion
  530.0 6.0 %copy.103 = f32[1152,1024]{1,0:T(8,128)} copy(f32[1152,1024]{0,1:T(8,128)} %slice_bitcast_fusion) | data formatting | bytes 9437184
  538.7 6.7 %fusion.73 = (f32[1024,1152]{1,0:T(8,128)}, f32[1024,1152]{1,0:T(8,128)}) fusion(bf16[1024,4224]{1,0:T(8,128)(2,1)} %get-tuple-element.16), kind=kLoop, calls=%fused_computation.170 | loop fusion | bytes 18874368 | tf_op jit(solution)/shard_map/slice | solution.py:563
  545.5 2.2 fusion.74
  547.6 2.1 slice.112
  552.1 9.8 %shard_map.239 = f32[32,1024]{1,0:T(8,128)} custom-call(bf16[128,1024]{1,0:T(8,128)(2,1)} %convolution_convert_fusion.7.whole_ref), custom_call_target="tpu_custom_call" | custom-call | tf_op jit(solution)/shard_map/pallas_call | solution.py:127
  562.0 1.7 fusion.44
  (177 shorter events, 44.3 us)
Async XLA Ops:
  0.6 126.4 %copy-start = (bf16[1152,1024]{1,0:T(8,128)(2,1)S(1)}, bf16[1152,1024]{1,0:T(8,128)(2,1)}, u32[]{:S(2)}) copy-start(bf16[1152,1024]{1,0:T(8,128)(2,1)} %param.26) | copy-start | bytes 7077892
  1.8 0.9 copy-start.47
  10.9 53.4 %copy-start.2 = (bf16[128,1024]{1,0:T(8,128)(2,1)}, bf16[128,1024]{1,0:T(8,128)(2,1)S(1)}, u32[]{:S(2)}) copy-start(bf16[128,1024]{1,0:T(8,128)(2,1)S(1)} %all_gather.12) | copy-start | bytes 786436
  12.2 0.6 copy-start.27
  12.8 3.8 copy-start.44
  16.8 47.4 %copy-start.32 = (f32[128,32]{0,1:T(8,128)}, f32[128,32]{0,1:T(8,128)S(1)}, u32[]{:S(2)}) copy-start(f32[128,32]{0,1:T(8,128)S(1)} %get-tuple-element.96) | copy-start | bytes 49156
  68.8 9.8 %copy-start.13 = (f32[128,256]{0,1:T(8,128)}, f32[128,256]{0,1:T(8,128)S(1)}, u32[]{:S(2)}) copy-start(f32[128,256]{0,1:T(8,128)S(1)} %copy.78) | copy-start | bytes 393220
  68.8 2.1 copy-start.40
  80.8 8.0 %copy-start.12 = (pred[64,2048]{1,0:T(8,128)(4,1)}, pred[64,2048]{1,0:T(8,128)(4,1)S(1)}, u32[]{:S(2)}) copy-start(pred[64,2048]{1,0:T(8,128)(4,1)S(1)} %broadcast_compare_fusion) | copy-start | bytes 393220
  82.9 2.0 copy-start.1
  82.9 3.1 copy-start.39
  86.0 0.6 copy-start.42
  96.1 2.0 copy-start.31
  96.1 23.5 %copy-start.29 = (bf16[32,1024]{1,0:T(8,128)(2,1)S(1)}, bf16[32,1024]{1,0:T(8,128)(2,1)}, u32[]{:S(2)}) copy-start(bf16[32,1024]{1,0:T(8,128)(2,1)} %param.27) | copy-start | bytes 196612
  107.3 11.7 %copy-start.5 = (bf16[1024,1152]{1,0:T(8,128)(2,1)S(1)}, bf16[1024,1152]{1,0:T(8,128)(2,1)}, u32[]{:S(2)}) copy-start(bf16[1024,1152]{1,0:T(8,128)(2,1)} %param.25) | copy-start | bytes 7077892
  108.5 33.4 %copy-start.45 = (f32[32]{0:T(128)}, f32[32]{0:T(128)S(1)}, u32[]{:S(2)}) copy-start(f32[32]{0:T(128)S(1)} %add_rsqrt_fusion.2) | copy-start | bytes 388
  116.7 2.3 copy-start.7
  119.0 9.8 %copy-start.4 = (bf16[1024,1152]{1,0:T(8,128)(2,1)S(1)}, bf16[1024,1152]{1,0:T(8,128)(2,1)}, u32[]{:S(2)}) copy-start(bf16[1024,1152]{1,0:T(8,128)(2,1)} %param.24) | copy-start | bytes 7077892
  127.1 2.6 copy-start.25
  128.8 0.9 copy-start.17
  128.8 0.9 copy-start.21
  128.8 11.5 %copy-start.35 = (f32[1024]{0:T(1024)S(1)}, f32[1024]{0:T(1024)}, u32[]{:S(2)}) copy-start(f32[1024]{0:T(1024)} %param.23) | copy-start | bytes 12292
  128.8 22.3 %copy-start.14 = (bf16[256,1024]{1,0:T(8,128)(2,1)S(1)}, bf16[256,1024]{1,0:T(8,128)(2,1)}, u32[]{:S(2)}) copy-start(bf16[256,1024]{1,0:T(8,128)(2,1)} %param.22) | copy-start | bytes 1572868
  141.9 8.5 %copy-start.51 = (f32[32]{0:T(128)}, f32[32]{0:T(128)S(1)}, u32[]{:S(2)}) copy-start(f32[32]{0:T(128)S(1)} %broadcast_multiply_fusion.3) | copy-start | bytes 388
  150.4 0.7 copy-start.9
  156.4 5.7 %copy-start.23 = (bf16[2,64,2,2,32]{4,1,3,2,0:T(8,128)(2,1)S(1)}, bf16[2,64,2,2,32]{4,1,3,2,0:T(8,128)(2,1)}, u32[]{:S(2)}) copy-start(bf16[2,64,2,2,32]{4,1,3,2,0:T(8,128)(2,1)} %copy.79) | copy-start | bytes 98308
  156.4 5.7 %copy-start.24 = (bf16[2,64,2,2,32]{4,1,3,2,0:T(8,128)(2,1)S(1)}, bf16[2,64,2,2,32]{4,1,3,2,0:T(8,128)(2,1)}, u32[]{:S(2)}) copy-start(bf16[2,64,2,2,32]{4,1,3,2,0:T(8,128)(2,1)} %copy.80) | copy-start | bytes 98308
  160.8 1.3 copy-start.6
  241.5 10.8 %copy-start.33 = (bf16[128,128]{0,1:T(8,128)(2,1)S(1)}, bf16[128,128]{0,1:T(8,128)(2,1)}, u32[]{:S(2)}) copy-start(bf16[128,128]{0,1:T(8,128)(2,1)} %get-tuple-element.80) | copy-start | bytes 98308
  241.5 12.0 %copy-start.28 = (f32[128,256]{1,0:T(8,128)S(1)}, f32[128,256]{1,0:T(8,128)}, u32[]{:S(2)}) copy-start(f32[128,256]{1,0:T(8,128)} %shard_map.241) | copy-start | bytes 393220
  241.5 22.9 %copy-start.15 = (bf16[32,1024]{1,0:T(8,128)(2,1)S(1)}, bf16[32,1024]{1,0:T(8,128)(2,1)}, u32[]{:S(2)}) copy-start(bf16[32,1024]{1,0:T(8,128)(2,1)} %param.14) | copy-start | bytes 196612
  241.5 22.9 %copy-start.37 = (f32[1024]{0:T(1024)S(1)}, f32[1024]{0:T(1024)}, u32[]{:S(2)}) copy-start(f32[1024]{0:T(1024)} %param.16) | copy-start | bytes 12292
  241.5 22.9 %copy-start.48 = (f32[32]{0:T(128)S(1)}, f32[32]{0:T(128)}, u32[]{:S(2)}) copy-start(f32[32]{0:T(128)} %copy-done.47) | copy-start | bytes 388
  241.6 24.0 %copy-start.53 = (f32[128]{0:T(128)S(1)}, f32[128]{0:T(128)}, u32[]{:S(2)}) copy-start(f32[128]{0:T(128)} %get-tuple-element.79) | copy-start | bytes 1540
  241.6 24.2 %copy-start.41 = (f32[1024]{0:T(1024)S(1)}, f32[1024]{0:T(1024)}, u32[]{:S(2)}) copy-start(f32[1024]{0:T(1024)} %get-tuple-element.56) | copy-start | bytes 12292
  241.6 31.8 %copy-start.50 = (pred[8,384]{1,0:T(8,128)(4,1)S(1)}, pred[8,384]{1,0:T(8,128)(4,1)}, u32[]{:S(2)}) copy-start(pred[8,384]{1,0:T(8,128)(4,1)} %constant.124.clone.1) | copy-start | bytes 9220
  241.6 33.1 %copy-start.3 = (bf16[128,1024]{1,0:T(8,128)(2,1)S(1)}, bf16[128,1024]{1,0:T(8,128)(2,1)}, u32[]{:S(2)}) copy-start(bf16[128,1024]{1,0:T(8,128)(2,1)} %copy-done.2) | copy-start | bytes 786436
  242.7 37.6 %copy-start.10 = (bf16[128,1024]{1,0:T(8,128)(2,1)S(1)}, bf16[128,1024]{1,0:T(8,128)(2,1)}, u32[]{:S(2)}) copy-start(bf16[128,1024]{1,0:T(8,128)(2,1)} %copy-done.9) | copy-start | bytes 786436
  245.3 37.1 %copy-start.8 = (bf16[128,1024]{1,0:T(8,128)(2,1)S(1)}, bf16[128,1024]{1,0:T(8,128)(2,1)}, u32[]{:S(2)}) copy-start(bf16[128,1024]{1,0:T(8,128)(2,1)} %copy-done.7) | copy-start | bytes 786436
  250.3 0.6 copy-start.34
  265.9 19.8 %copy-start.22 = (bf16[128,1152]{1,0:T(8,128)(2,1)S(1)}, bf16[128,1152]{1,0:T(8,128)(2,1)}, u32[]{:S(2)}) copy-start(bf16[128,1152]{1,0:T(8,128)(2,1)} %copy-done.21) | copy-start | bytes 884740
  274.7 13.3 %copy-start.19 = (bf16[128,1152]{1,0:T(8,128)(2,1)S(1)}, bf16[128,1152]{1,0:T(8,128)(2,1)}, u32[]{:S(2)}) copy-start(bf16[128,1152]{1,0:T(8,128)(2,1)} %get-tuple-element.72) | copy-start | bytes 884740
  274.7 13.3 %copy-start.26 = (bf16[128,1024]{1,0:T(8,128)(2,1)S(1)}, bf16[128,1024]{1,0:T(8,128)(2,1)}, u32[]{:S(2)}) copy-start(bf16[128,1024]{1,0:T(8,128)(2,1)} %copy-done.25) | copy-start | bytes 786436
  545.4 4.3 copy-start.43
  545.4 5.5 copy-start.20
  545.4 16.5 %copy-start.11 = (f32[32,1024]{1,0:T(8,128)S(1)}, f32[32,1024]{1,0:T(8,128)}, u32[]{:S(2)}) copy-start(f32[32,1024]{1,0:T(8,128)} %shard_map.240) | copy-start | bytes 393220
  545.4 16.5 %copy-start.16 = (bf16[32,1024]{1,0:T(8,128)(2,1)S(1)}, bf16[32,1024]{1,0:T(8,128)(2,1)}, u32[]{:S(2)}) copy-start(bf16[32,1024]{1,0:T(8,128)(2,1)} %param.14) | copy-start | bytes 196612
  545.4 16.5 %copy-start.18 = (f32[32,1024]{1,0:T(8,128)S(1)}, f32[32,1024]{1,0:T(8,128)}, u32[]{:S(2)}) copy-start(f32[32,1024]{1,0:T(8,128)} %shard_map.242) | copy-start | bytes 393220
  545.4 16.5 %copy-start.30 = (bf16[32,1024]{1,0:T(8,128)(2,1)S(1)}, bf16[32,1024]{1,0:T(8,128)(2,1)}, u32[]{:S(2)}) copy-start(bf16[32,1024]{1,0:T(8,128)(2,1)} %param.27) | copy-start | bytes 196612
  545.4 16.5 %copy-start.36 = (f32[1024]{0:T(1024)S(1)}, f32[1024]{0:T(1024)}, u32[]{:S(2)}) copy-start(f32[1024]{0:T(1024)} %param.23) | copy-start | bytes 12292
  545.4 16.5 %copy-start.38 = (f32[1024]{0:T(1024)S(1)}, f32[1024]{0:T(1024)}, u32[]{:S(2)}) copy-start(f32[1024]{0:T(1024)} %param.16) | copy-start | bytes 12292
  545.4 16.5 %copy-start.46 = (f32[32]{0:T(128)S(1)}, f32[32]{0:T(128)}, u32[]{:S(2)}) copy-start(f32[32]{0:T(128)} %copy-done.45) | copy-start | bytes 388
  545.5 16.5 %copy-start.49 = (f32[32]{0:T(128)S(1)}, f32[32]{0:T(128)}, u32[]{:S(2)}) copy-start(f32[32]{0:T(128)} %copy-done.47) | copy-start | bytes 388
  545.5 16.5 %copy-start.52 = (f32[32]{0:T(128)S(1)}, f32[32]{0:T(128)}, u32[]{:S(2)}) copy-start(f32[32]{0:T(128)} %copy-done.51) | copy-start | bytes 388

commit v5 on v4

--- a/solution.py
+++ b/solution.py
@@ -145,7 +145,7 @@
     return jnp.where(step % 2 == 0, half, n - half)
 
 
-def _sum_kernel(n, spans, whole_ref, extra_ref, out_ref, extra_out, *scratch):
+def _sum_kernel(n, spans, whole_ref, extra_ref, out_ref, extra_out, wide_out, *scratch):
     pieces = len(spans)
     helds, mines, extra_held = scratch[:pieces], scratch[pieces : 2 * pieces], scratch[2 * pieces]
     sems = scratch[2 * pieces + 1 :]
@@ -241,6 +241,8 @@
             return carry
 
         each_peer(finish)
+        first, width = spans[piece]
+        wide_out[:, pl.ds(first, width)] = out_ref[:, pl.ds(first, width)].astype(wide_out.dtype)
 
     def finish_extra(k, target, source, carry):
         extra_copy(k, target).wait_send()
@@ -259,9 +261,10 @@
         out_shape=(
             jax.ShapeDtypeStruct(whole.shape, whole.dtype),
             jax.ShapeDtypeStruct(extra.shape, extra.dtype),
+            jax.ShapeDtypeStruct(whole.shape, jnp.float32),
         ),
         in_specs=[pl.BlockSpec(memory_space=pltpu.VMEM)] * 2,
-        out_specs=(pl.BlockSpec(memory_space=pltpu.VMEM),) * 2,
+        out_specs=(pl.BlockSpec(memory_space=pltpu.VMEM),) * 3,
         scratch_shapes=[pltpu.VMEM((n, rows, width), whole.dtype) for _, width in spans]
         + [pltpu.VMEM((rows, width), whole.dtype) for _, width in spans]
         + [pltpu.VMEM((n,) + extra.shape, extra.dtype)]
@@ -550,13 +553,12 @@
         7,
         "tp",
     ).reshape(-1)[: gain_local.shape[0]]
-    summed, gains = ctx_sum(
+    _, gains, summed = ctx_sum(
         jnp.concatenate([part.astype(jnp.bfloat16) for part in weight_parts], axis=1),
         jnp.pad(gain_flat, (0, gain_pad)).reshape(8, -1),
         place_count,
         2,
     )
-    summed = summed.astype(jnp.float32)
     gains = gains.reshape(-1)
     offsets = [sum(widths[:k]) for k in range(len(widths) + 1)]
     shared_query, shared_key, shared_value, output_t, shared_gate, shared_up, down_t = (

time: 570 us -> 527 us (0.925)
  local copies, waits for them, and re-layouts: 79.3 us -> 57.1 us
  other arithmetic: 45.4 us -> 26.1 us
  matrix products: 55.1 us -> 45.7 us
  Pallas kernels: 351 us -> 357 us
    convert_element_type x1 -> x0, other arithmetic: 10.5 us -> none  [per_device(): summed = summed.astype(jnp.float32)]
    slice x3 -> x1, local copies, waits for them, and re-layouts: 11 us -> 2.24 us  [per_device(): summed[:, offsets[k]:offsets[k + 1]]]
    transpose x1, local copies, waits for them, and re-layouts: 4.82 us -> 10.6 us  [per_device(): shared_down = down_t.T]
    unnamed x110 -> x108, local copies, waits for them, and re-layouts: 12.8 us -> 9.04 us
where the time goes in v5:
time: 527 us; the launch traced here: 519 us
  Pallas kernels  357 us (68%)
  local copies, waits for them, and re-layouts  57.1 us (11%)
  matrix products  45.7 us (9%)
  blocking collectives  30.8 us (6%)
  other arithmetic  26.1 us (5%)
    pallas_call x1, Pallas kernels, ctx_sum(): pl.pallas_call(functools.partial(_sum_kernel, n, spans), out_shape=(jax.S...  230 us
    pallas_call x6, Pallas kernels, ctx_scatter(): pl.pallas_call(functools.partial(_scatter_kernel, n, axis), out_shape=jax...  85.2 us
    pallas_call x1, Pallas kernels, ctx_gather(): pl.pallas_call(functools.partial(_gather_kernel, n), out_shape=jax.ShapeD...  42 us
    all_gather x4, blocking collectives, gather_rows(): return lax.all_gather(rows_low, 'tp', axis=0, tiled=True)  30.8 us
    transpose x1, local copies, waits for them, and re-layouts, per_device(): shared_down = down_t.T  10.6 us

profile of v5, /device:TPU:28, one launch (start us, length us, event | category | flops | bytes accessed | tf_op | source)
XLA Modules:
  0.0 518.8 jit_solution(18339686632480964856)
XLA Ops:
  0.7 1.5 fusion.61
  4.2 1.0 fusion.49
  8.1 0.9 fusion.40
  9.2 8.1 %all_gather.12 = bf16[128,1024]{1,0:T(8,128)(2,1)S(1)} all-gather(bf16[32,1024]{1,0:T(8,128)(2,1)S(1)} %fusion.40), channel_id=1, replica_groups=mesh['ctx'=32,'tp'=4] {'tp'}, dimensions={0}, use_global_device_ids=true | all-gather | bytes 327680 | tf_op jit(solution)/shard_map/all_gather | solution.py:357
  17.3 1.3 convolution_convert_fusion.10
  18.6 1.2 multiply_reduce_fusion.8
  21.4 1.3 fusion.78
  26.2 7.8 %all_gather.14 = bf16[128,1024]{1,0:T(8,128)(2,1)} all-gather(bf16[32,1024]{1,0:T(8,128)(2,1)S(1)} %copy-done.31), channel_id=1, replica_groups=mesh['ctx'=32,'tp'=4] {'tp'}, dimensions={0}, use_global_device_ids=true | all-gather | bytes 327680 | tf_op jit(solution)/shard_map/all_gather | solution.py:357
  34.0 42.0 %shard_map.237 = bf16[4096,256]{1,0:T(8,128)(2,1)} custom-call(bf16[128,256]{1,0:T(8,128)(2,1)} %pad_maximum_fusion.2.part_ref), custom_call_target="tpu_custom_call" | custom-call | tf_op jit(solution)/shard_map/pallas_call | solution.py:74
  76.0 1.7 copy.76
  77.8 1.7 fusion.74
  79.4 1.5 copy.77
  80.9 2.3 copy.81
  83.2 2.0 fusion.2
  85.3 1.1 fusion.12
  86.4 0.8 log_add_fusion
  87.2 2.0 fusion.77
  89.2 1.7 copy.82
  90.9 1.1 convert_element_type.120
  92.0 2.0 convolution_convert_fusion.8.whole_ref
  94.0 9.2 %shard_map.238 = f32[32,1024]{1,0:T(8,128)} custom-call(bf16[128,1024]{1,0:T(8,128)(2,1)} %convolution_convert_fusion.8.whole_ref), custom_call_target="tpu_custom_call" | custom-call | tf_op jit(solution)/shard_map/pallas_call | solution.py:127
  103.2 1.2 multiply_reduce_fusion.5
  105.2 7.4 %all_gather.13 = bf16[128,1024]{1,0:T(8,128)(2,1)S(1)} all-gather(bf16[32,1024]{1,0:T(8,128)(2,1)S(1)} %multiply_convert_fusion.3), channel_id=1, replica_groups=mesh['ctx'=32,'tp'=4] {'tp'}, dimensions={0}, use_global_device_ids=true | all-gather | bytes 327680 | tf_op jit(solution)/shard_map/all_gather | solution.py:357
  112.6 2.3 fusion.80
  115.4 1.8 multiply_convert_fusion
  118.0 1.2 convolution_convert_fusion.7.whole_ref
  119.2 9.1 %shard_map.239 = f32[32,1024]{1,0:T(8,128)} custom-call(bf16[128,1024]{1,0:T(8,128)(2,1)} %convolution_convert_fusion.7.whole_ref), custom_call_target="tpu_custom_call" | custom-call | tf_op jit(solution)/shard_map/pallas_call | solution.py:127
  128.3 2.7 fusion.81
  131.0 3.4 fusion.31.whole_ref
  134.3 9.0 %shard_map.240 = f32[32,1024]{1,0:T(8,128)} custom-call(bf16[128,1024]{1,0:T(8,128)(2,1)} %fusion.31.whole_ref), custom_call_target="tpu_custom_call" | custom-call | tf_op jit(solution)/shard_map/pallas_call | solution.py:127
  143.4 1.6 multiply_reduce_fusion.1
  145.0 1.0 fusion.70
  146.0 7.5 %all_gather.15 = bf16[128,1024]{1,0:T(8,128)(2,1)S(1)} all-gather(bf16[32,1024]{1,0:T(8,128)(2,1)S(1)} %fusion.70), channel_id=1, replica_groups=mesh['ctx'=32,'tp'=4] {'tp'}, dimensions={0}, use_global_device_ids=true | all-gather | bytes 327680 | tf_op jit(solution)/shard_map/all_gather | solution.py:357
  154.7 4.5 fusion.1
  159.2 2.1 fusion.16
  161.3 1.1 convolution_bitcast_fusion.2
  164.2 1.0 pad_maximum_fusion.1
  165.4 1.0 multiply_reduce_fusion.2
  167.1 2.1 fusion.82
  169.2 2.2 reshape.336
  171.4 4.4 reshape.337
  175.8 4.4 maximum_bitcast_fusion
  180.3 5.5 %copy.93 = bf16[32,2,64,256]{3,2,1,0:T(8,128)(2,1)} copy(bf16[32,2,64,256]{2,0,3,1:T(8,128)(2,1)} %maximum_bitcast_fusion) | data formatting | bytes 4194304 | tf_op jit(solution)/shard_map/convert_element_type | solution.py:511
  185.8 41.4 %shard_map.241 = f32[128,256]{1,0:T(8,128)} custom-call(bf16[4096,256]{1,0:T(8,128)(2,1)} %bitcast.193), custom_call_target="tpu_custom_call" | custom-call | tf_op jit(solution)/shard_map/pallas_call | solution.py:127
  227.3 0.9 slice.85
  228.9 1.8 fusion.28.whole_ref
  230.7 9.8 %shard_map.242 = f32[32,1024]{1,0:T(8,128)} custom-call(bf16[128,1024]{1,0:T(8,128)(2,1)} %fusion.28.whole_ref), custom_call_target="tpu_custom_call" | custom-call | tf_op jit(solution)/shard_map/pallas_call | solution.py:127
  240.6 1.1 fusion.52
  241.7 1.7 fusion.44
  244.9 6.8 %shard_map.243 = f32[8,384]{1,0:T(8,128)} custom-call(f32[32,384]{1,0:T(8,128)} %broadcast_bitcast_fusion.whole_ref), custom_call_target="tpu_custom_call" | custom-call | tf_op jit(solution)/shard_map/pallas_call | solution.py:127
  251.7 1.3 broadcast_select_fusion.extra_ref
  253.1 1.2 fusion.27
  254.2 1.0 fusion.30
  255.2 1.0 fusion.29
  256.2 1.2 fusion.26
  257.4 2.3 fusion.8
  259.7 2.3 fusion.7
  262.0 2.3 fusion.10.whole_ref
  264.3 229.6 %shard_map.244 = (bf16[1024,4224]{1,0:T(8,128)(2,1)}, f32[8,384]{1,0:T(8,128)}, f32[1024,4224]{1,0:T(8,128)}) custom-call(bf16[1024,4224]{1,0:T(8,128)(2,1)} %fusion.10.whole_ref, f32[8,384]{1,0:T(8,128)} %broadcast_select_fusion.extra_ref), custom_call_target="tpu_custom_call" | custom-call | tf_op jit(solution)/shard_map/pallas_call | solution.py:259
  495.8 2.2 fusion.73
  498.0 2.7 slice_bitcast_fusion.1
  500.7 10.6 %slice_bitcast_fusion = (f32[1152,1024]{0,1:T(8,128)}, f32[1024,1152]{1,0:T(8,128)}, f32[1024,1152]{1,0:T(8,128)}) fusion(f32[1024,4224]{1,0:T(8,128)} %get-tuple-element.16), kind=kLoop, calls=%fused_computation | loop fusion | bytes 28311552 | tf_op jit(solution)/shard_map/transpose | solution.py:568
  511.2 6.2 %copy.103 = f32[1152,1024]{1,0:T(8,128)} copy(f32[1152,1024]{0,1:T(8,128)} %get-tuple-element.64) | data formatting | bytes 9437184
  517.4 1.3 copy.102
  (172 shorter events, 19.3 us)
Async XLA Ops:
  0.6 114.8 %copy-start = (bf16[1152,1024]{1,0:T(8,128)(2,1)S(1)}, bf16[1152,1024]{1,0:T(8,128)(2,1)}, u32[]{:S(2)}) copy-start(bf16[1152,1024]{1,0:T(8,128)(2,1)} %param.26) | copy-start | bytes 7077892
  0.7 25.5 %copy-start.31 = (bf16[32,1024]{1,0:T(8,128)(2,1)S(1)}, bf16[32,1024]{1,0:T(8,128)(2,1)}, u32[]{:S(2)}) copy-start(bf16[32,1024]{1,0:T(8,128)(2,1)} %param.27) | copy-start | bytes 196612
  5.2 4.0 copy-start.48
  8.1 69.6 %copy-start.39 = (f32[128,32]{0,1:T(8,128)}, f32[128,32]{0,1:T(8,128)S(1)}, u32[]{:S(2)}) copy-start(f32[128,32]{0,1:T(8,128)S(1)} %get-tuple-element.99) | copy-start | bytes 49156
  9.2 78.0 %copy-start.10 = (pred[64,2048]{1,0:T(8,128)(4,1)}, pred[64,2048]{1,0:T(8,128)(4,1)S(1)}, u32[]{:S(2)}) copy-start(pred[64,2048]{1,0:T(8,128)(4,1)S(1)} %broadcast_compare_fusion) | copy-start | bytes 393220
  17.3 60.4 %copy-start.4 = (bf16[128,1024]{1,0:T(8,128)(2,1)}, bf16[128,1024]{1,0:T(8,128)(2,1)S(1)}, u32[]{:S(2)}) copy-start(bf16[128,1024]{1,0:T(8,128)(2,1)S(1)} %all_gather.12) | copy-start | bytes 786436
  19.8 1.6 copy-start.26
  19.9 0.8 copy-start.45
  22.7 55.0 %copy-start.17 = (f32[128,256]{1,0:T(8,128)}, f32[128,256]{1,0:T(8,128)S(1)}, u32[]{:S(2)}) copy-start(f32[128,256]{1,0:T(8,128)S(1)} %fusion.78) | copy-start | bytes 393220
  22.8 56.6 %copy-start.12 = (f32[128,256]{0,1:T(8,128)}, f32[128,256]{0,1:T(8,128)S(1)}, u32[]{:S(2)}) copy-start(f32[128,256]{0,1:T(8,128)S(1)} %copy.78) | copy-start | bytes 393220
  83.2 4.0 copy-start.28
  85.2 4.0 copy-start.2
  92.0 2.0 copy-start.34
  92.0 23.4 %copy-start.23 = (bf16[128,1024]{1,0:T(8,128)(2,1)S(1)}, bf16[128,1024]{1,0:T(8,128)(2,1)}, u32[]{:S(2)}) copy-start(bf16[128,1024]{1,0:T(8,128)(2,1)} %all_gather.14) | copy-start | bytes 786436
  103.2 11.7 %copy-start.6 = (bf16[1024,1152]{1,0:T(8,128)(2,1)S(1)}, bf16[1024,1152]{1,0:T(8,128)(2,1)}, u32[]{:S(2)}) copy-start(bf16[1024,1152]{1,0:T(8,128)(2,1)} %param.24) | copy-start | bytes 7077892
  104.4 40.5 %copy-start.47 = (f32[32]{0:T(128)}, f32[32]{0:T(128)S(1)}, u32[]{:S(2)}) copy-start(f32[32]{0:T(128)S(1)} %add_rsqrt_fusion.2) | copy-start | bytes 388
  112.6 2.3 copy-start.7
  117.2 0.7 copy-start.18
  119.2 24.2 %copy-start.44 = (f32[1024]{0:T(1024)S(1)}, f32[1024]{0:T(1024)}, u32[]{:S(2)}) copy-start(f32[1024]{0:T(1024)} %param.23) | copy-start | bytes 12292
  119.2 25.8 %copy-start.32 = (bf16[32,1024]{1,0:T(8,128)(2,1)S(1)}, bf16[32,1024]{1,0:T(8,128)(2,1)}, u32[]{:S(2)}) copy-start(bf16[32,1024]{1,0:T(8,128)(2,1)} %param.27) | copy-start | bytes 196612
  119.2 34.2 %copy-start.13 = (bf16[256,1024]{1,0:T(8,128)(2,1)S(1)}, bf16[256,1024]{1,0:T(8,128)(2,1)}, u32[]{:S(2)}) copy-start(bf16[256,1024]{1,0:T(8,128)(2,1)} %param.22) | copy-start | bytes 1572868
  128.3 25.7 %copy-start.43 = (f32[2,64,2,2,64]{1,4,3,2,0:T(8,128)S(1)}, f32[2,64,2,2,64]{1,4,3,2,0:T(8,128)}, u32[]{:S(2)}) copy-start(f32[2,64,2,2,64]{1,4,3,2,0:T(8,128)} %get-tuple-element.105) | copy-start | bytes 393220
  144.9 8.5 %copy-start.50 = (f32[32]{0:T(128)}, f32[32]{0:T(128)S(1)}, u32[]{:S(2)}) copy-start(f32[32]{0:T(128)S(1)} %broadcast_multiply_fusion.3) | copy-start | bytes 388
  154.0 0.7 copy-start.37
  154.7 4.5 copy-start.3
  154.7 4.5 copy-start.11
  154.7 4.5 copy-start.38
  154.7 4.5 copy-start.49
  159.2 3.3 copy-start.21
  159.2 3.2 copy-start.22
  166.4 0.6 copy-start.41
  180.2 48.1 %copy-start.40 = (f32[128,32]{0,1:T(8,128)S(1)}, f32[128,32]{0,1:T(8,128)}, u32[]{:S(2)}) copy-start(f32[128,32]{0,1:T(8,128)} %copy-done.39) | copy-start | bytes 49156
  180.2 48.1 %copy-start.27 = (f32[128,128]{0,1:T(8,128)S(1)}, f32[128,128]{0,1:T(8,128)}, u32[]{:S(2)}) copy-start(f32[128,128]{0,1:T(8,128)} %copy-done.26) | copy-start | bytes 196612
  180.2 48.1 %copy-start.51 = (f32[64]{0:T(128)S(1)}, f32[64]{0:T(128)}, u32[]{:S(2)}) copy-start(f32[64]{0:T(128)} %param.21) | copy-start | bytes 772
  180.2 48.2 %copy-start.46 = (f32[128,2]{0,1:T(2,128)S(1)}, f32[128,2]{0,1:T(2,128)}, u32[]{:S(2)}) copy-start(f32[128,2]{0,1:T(2,128)} %copy-done.45) | copy-start | bytes 3076
  180.2 48.2 %copy-start.52 = (f32[128]{0:T(128)S(1)}, f32[128]{0:T(128)}, u32[]{:S(2)}) copy-start(f32[128]{0:T(128)} %mul.551) | copy-start | bytes 1540
  180.2 48.4 %copy-start.14 = (f32[128,1024]{1,0:T(8,128)S(1)}, f32[128,1024]{1,0:T(8,128)}, u32[]{:S(2)}) copy-start(f32[128,1024]{1,0:T(8,128)} %fusion.82) | copy-start | bytes 1572868
  180.2 48.4 %copy-start.29 = (bf16[1024,128]{1,0:T(8,128)(2,1)S(1)}, bf16[1024,128]{1,0:T(8,128)(2,1)}, u32[]{:S(2)}) copy-start(bf16[1024,128]{1,0:T(8,128)(2,1)} %param.18) | copy-start | bytes 786436
  180.3 48.6 %copy-start.25 = (bf16[1024,128]{1,0:T(8,128)(2,1)S(1)}, bf16[1024,128]{1,0:T(8,128)(2,1)}, u32[]{:S(2)}) copy-start(bf16[1024,128]{1,0:T(8,128)(2,1)} %param.19) | copy-start | bytes 786436
  185.8 54.8 %copy-start.15 = (bf16[32,1024]{1,0:T(8,128)(2,1)S(1)}, bf16[32,1024]{1,0:T(8,128)(2,1)}, u32[]{:S(2)}) copy-start(bf16[32,1024]{1,0:T(8,128)(2,1)} %param.14) | copy-start | bytes 196612
  185.8 55.9 %copy-start.9 = (f32[32,1024]{1,0:T(8,128)S(1)}, f32[32,1024]{1,0:T(8,128)}, u32[]{:S(2)}) copy-start(f32[32,1024]{1,0:T(8,128)} %shard_map.240) | copy-start | bytes 393220
  185.8 55.9 %copy-start.33 = (bf16[32,1024]{1,0:T(8,128)(2,1)S(1)}, bf16[32,1024]{1,0:T(8,128)(2,1)}, u32[]{:S(2)}) copy-start(bf16[32,1024]{1,0:T(8,128)(2,1)} %param.27) | copy-start | bytes 196612
  185.8 55.9 %copy-start.36 = (f32[32,1024]{1,0:T(8,128)S(1)}, f32[32,1024]{1,0:T(8,128)}, u32[]{:S(2)}) copy-start(f32[32,1024]{1,0:T(8,128)} %shard_map.239) | copy-start | bytes 393220
  185.8 67.2 %copy-start.5 = (bf16[128,1024]{1,0:T(8,128)(2,1)S(1)}, bf16[128,1024]{1,0:T(8,128)(2,1)}, u32[]{:S(2)}) copy-start(bf16[128,1024]{1,0:T(8,128)(2,1)} %copy-done.4) | copy-start | bytes 786436
  185.8 67.2 %copy-start.42 = (bf16[128,256]{1,0:T(8,128)(2,1)S(1)}, bf16[128,256]{1,0:T(8,128)(2,1)}, u32[]{:S(2)}) copy-start(bf16[128,256]{1,0:T(8,128)(2,1)} %copy-done.41) | copy-start | bytes 196612
  185.8 70.4 %copy-start.35 = (bf16[128,256]{1,0:T(8,128)(2,1)S(1)}, bf16[128,256]{1,0:T(8,128)(2,1)}, u32[]{:S(2)}) copy-start(bf16[128,256]{1,0:T(8,128)(2,1)} %copy-done.34) | copy-start | bytes 196612
  227.3 28.0 %copy-start.30 = (f32[128,256]{1,0:T(8,128)S(1)}, f32[128,256]{1,0:T(8,128)}, u32[]{:S(2)}) copy-start(f32[128,256]{1,0:T(8,128)} %shard_map.241) | copy-start | bytes 393220
  227.3 30.1 %copy-start.8 = (bf16[128,1024]{1,0:T(8,128)(2,1)S(1)}, bf16[128,1024]{1,0:T(8,128)(2,1)}, u32[]{:S(2)}) copy-start(bf16[128,1024]{1,0:T(8,128)(2,1)} %copy-done.7) | copy-start | bytes 786436
  227.3 30.1 %copy-start.16 = (bf16[128,1152]{1,0:T(8,128)(2,1)S(1)}, bf16[128,1152]{1,0:T(8,128)(2,1)}, u32[]{:S(2)}) copy-start(bf16[128,1152]{1,0:T(8,128)(2,1)} %get-tuple-element.74) | copy-start | bytes 884740
  228.9 30.8 %copy-start.20 = (bf16[128,1152]{1,0:T(8,128)(2,1)S(1)}, bf16[128,1152]{1,0:T(8,128)(2,1)}, u32[]{:S(2)}) copy-start(bf16[128,1152]{1,0:T(8,128)(2,1)} %get-tuple-element.73) | copy-start | bytes 884740
  253.1 8.9 %copy-start.19 = (bf16[128,1152]{1,0:T(8,128)(2,1)S(1)}, bf16[128,1152]{1,0:T(8,128)(2,1)}, u32[]{:S(2)}) copy-start(bf16[128,1152]{1,0:T(8,128)(2,1)} %copy-done.18) | copy-start | bytes 884740
  253.1 8.9 %copy-start.24 = (bf16[128,1024]{1,0:T(8,128)(2,1)S(1)}, bf16[128,1024]{1,0:T(8,128)(2,1)}, u32[]{:S(2)}) copy-start(bf16[128,1024]{1,0:T(8,128)(2,1)} %all_gather.14) | copy-start | bytes 786436
  511.2 7.5 %copy-start.1 = (bf16[1152,1024]{1,0:T(8,128)(2,1)S(1)}, bf16[1152,1024]{1,0:T(8,128)(2,1)}, u32[]{:S(2)}) copy-start(bf16[1152,1024]{1,0:T(8,128)(2,1)} %param.26) | copy-start | bytes 7077892

commit v6 on v5

--- a/solution.py
+++ b/solution.py
@@ -251,7 +251,7 @@
     each_peer(finish_extra)
 
 
-def ctx_sum(whole, extra, n, collective_id, pieces=8):
+def ctx_sum(whole, extra, n, collective_id, pieces=11):
     rows, cols = whole.shape[0] // n, whole.shape[1]
     lanes = cols // 128
     edges = [128 * (lanes * p // pieces) for p in range(pieces + 1)]

time: 527 us -> 521 us (0.989)
  Pallas kernels: 357 us -> 349 us
    pallas_call x1, Pallas kernels: 230 us -> 222 us  [ctx_sum(): pl.pallas_call(functools.partial(_sum_kernel, n, spans), out_shape=(jax.S...]
where the time goes in v6:
time: 521 us; the launch traced here: 511 us
  Pallas kernels  349 us (67%)
  local copies, waits for them, and re-layouts  57.1 us (11%)
  matrix products  45.7 us (9%)
  blocking collectives  30.8 us (6%)
  other arithmetic  26.1 us (5%)
    pallas_call x1, Pallas kernels, ctx_sum(): pl.pallas_call(functools.partial(_sum_kernel, n, spans), out_shape=(jax.S...  222 us
    pallas_call x6, Pallas kernels, ctx_scatter(): pl.pallas_call(functools.partial(_scatter_kernel, n, axis), out_shape=jax...  85.2 us
    pallas_call x1, Pallas kernels, ctx_gather(): pl.pallas_call(functools.partial(_gather_kernel, n), out_shape=jax.ShapeD...  42 us
    all_gather x4, blocking collectives, gather_rows(): return lax.all_gather(rows_low, 'tp', axis=0, tiled=True)  30.8 us
    transpose x1, local copies, waits for them, and re-layouts, per_device(): shared_down = down_t.T  10.6 us

profile of v6, /device:TPU:28, one launch (start us, length us, event | category | flops | bytes accessed | tf_op | source)
XLA Modules:
  0.0 511.3 jit_solution(825865042296696706)
XLA Ops:
  0.7 1.5 fusion.61
  4.2 1.0 fusion.49
  8.1 0.9 fusion.40
  9.2 8.1 %all_gather.12 = bf16[128,1024]{1,0:T(8,128)(2,1)S(1)} all-gather(bf16[32,1024]{1,0:T(8,128)(2,1)S(1)} %fusion.40), channel_id=1, replica_groups=mesh['ctx'=32,'tp'=4] {'tp'}, dimensions={0}, use_global_device_ids=true | all-gather | bytes 327680 | tf_op jit(solution)/shard_map/all_gather | solution.py:357
  17.3 1.3 convolution_convert_fusion.10
  18.6 1.2 multiply_reduce_fusion.8
  21.4 1.3 fusion.78
  26.2 7.8 %all_gather.14 = bf16[128,1024]{1,0:T(8,128)(2,1)} all-gather(bf16[32,1024]{1,0:T(8,128)(2,1)S(1)} %copy-done.31), channel_id=1, replica_groups=mesh['ctx'=32,'tp'=4] {'tp'}, dimensions={0}, use_global_device_ids=true | all-gather | bytes 327680 | tf_op jit(solution)/shard_map/all_gather | solution.py:357
  34.0 42.0 %shard_map.237 = bf16[4096,256]{1,0:T(8,128)(2,1)} custom-call(bf16[128,256]{1,0:T(8,128)(2,1)} %pad_maximum_fusion.2.part_ref), custom_call_target="tpu_custom_call" | custom-call | tf_op jit(solution)/shard_map/pallas_call | solution.py:74
  76.0 1.7 copy.76
  77.8 1.7 fusion.74
  79.4 1.5 copy.77
  80.9 2.3 copy.81
  83.2 2.0 fusion.2
  85.3 1.1 fusion.12
  86.4 0.8 log_add_fusion
  87.2 2.0 fusion.77
  89.2 1.7 copy.82
  90.9 1.1 convert_element_type.120
  92.0 2.0 convolution_convert_fusion.8.whole_ref
  94.0 9.2 %shard_map.238 = f32[32,1024]{1,0:T(8,128)} custom-call(bf16[128,1024]{1,0:T(8,128)(2,1)} %convolution_convert_fusion.8.whole_ref), custom_call_target="tpu_custom_call" | custom-call | tf_op jit(solution)/shard_map/pallas_call | solution.py:127
  103.2 1.2 multiply_reduce_fusion.5
  105.2 7.4 %all_gather.13 = bf16[128,1024]{1,0:T(8,128)(2,1)S(1)} all-gather(bf16[32,1024]{1,0:T(8,128)(2,1)S(1)} %multiply_convert_fusion.3), channel_id=1, replica_groups=mesh['ctx'=32,'tp'=4] {'tp'}, dimensions={0}, use_global_device_ids=true | all-gather | bytes 327680 | tf_op jit(solution)/shard_map/all_gather | solution.py:357
  112.6 2.3 fusion.80
  115.4 1.8 multiply_convert_fusion
  118.0 1.2 convolution_convert_fusion.7.whole_ref
  119.2 9.1 %shard_map.239 = f32[32,1024]{1,0:T(8,128)} custom-call(bf16[128,1024]{1,0:T(8,128)(2,1)} %convolution_convert_fusion.7.whole_ref), custom_call_target="tpu_custom_call" | custom-call | tf_op jit(solution)/shard_map/pallas_call | solution.py:127
  128.3 2.7 fusion.81
  131.0 3.4 fusion.31.whole_ref
  134.3 9.0 %shard_map.240 = f32[32,1024]{1,0:T(8,128)} custom-call(bf16[128,1024]{1,0:T(8,128)(2,1)} %fusion.31.whole_ref), custom_call_target="tpu_custom_call" | custom-call | tf_op jit(solution)/shard_map/pallas_call | solution.py:127
  143.4 1.6 multiply_reduce_fusion.1
  145.0 1.0 fusion.70
  146.0 7.5 %all_gather.15 = bf16[128,1024]{1,0:T(8,128)(2,1)S(1)} all-gather(bf16[32,1024]{1,0:T(8,128)(2,1)S(1)} %fusion.70), channel_id=1, replica_groups=mesh['ctx'=32,'tp'=4] {'tp'}, dimensions={0}, use_global_device_ids=true | all-gather | bytes 327680 | tf_op jit(solution)/shard_map/all_gather | solution.py:357
  154.7 4.5 fusion.1
  159.2 2.1 fusion.16
  161.3 1.1 convolution_bitcast_fusion.2
  164.2 1.0 pad_maximum_fusion.1
  165.4 1.0 multiply_reduce_fusion.2
  167.1 2.1 fusion.82
  169.2 2.2 reshape.336
  171.4 4.4 reshape.337
  175.8 4.4 maximum_bitcast_fusion
  180.3 5.5 %copy.93 = bf16[32,2,64,256]{3,2,1,0:T(8,128)(2,1)} copy(bf16[32,2,64,256]{2,0,3,1:T(8,128)(2,1)} %maximum_bitcast_fusion) | data formatting | bytes 4194304 | tf_op jit(solution)/shard_map/convert_element_type | solution.py:511
  185.8 41.4 %shard_map.241 = f32[128,256]{1,0:T(8,128)} custom-call(bf16[4096,256]{1,0:T(8,128)(2,1)} %bitcast.193), custom_call_target="tpu_custom_call" | custom-call | tf_op jit(solution)/shard_map/pallas_call | solution.py:127
  227.3 0.9 slice.85
  228.9 1.8 fusion.28.whole_ref
  230.7 9.8 %shard_map.242 = f32[32,1024]{1,0:T(8,128)} custom-call(bf16[128,1024]{1,0:T(8,128)(2,1)} %fusion.28.whole_ref), custom_call_target="tpu_custom_call" | custom-call | tf_op jit(solution)/shard_map/pallas_call | solution.py:127
  240.6 1.1 fusion.52
  241.7 1.7 fusion.44
  244.9 6.8 %shard_map.243 = f32[8,384]{1,0:T(8,128)} custom-call(f32[32,384]{1,0:T(8,128)} %broadcast_bitcast_fusion.whole_ref), custom_call_target="tpu_custom_call" | custom-call | tf_op jit(solution)/shard_map/pallas_call | solution.py:127
  251.7 1.3 broadcast_select_fusion.extra_ref
  253.1 1.2 fusion.27
  254.2 1.0 fusion.30
  255.2 1.0 fusion.29
  256.2 1.2 fusion.26
  257.4 2.3 fusion.8
  259.7 2.3 fusion.7
  262.0 2.3 fusion.10.whole_ref
  264.3 222.1 %shard_map.244 = (bf16[1024,4224]{1,0:T(8,128)(2,1)}, f32[8,384]{1,0:T(8,128)}, f32[1024,4224]{1,0:T(8,128)}) custom-call(bf16[1024,4224]{1,0:T(8,128)(2,1)} %fusion.10.whole_ref, f32[8,384]{1,0:T(8,128)} %broadcast_select_fusion.extra_ref), custom_call_target="tpu_custom_call" | custom-call | tf_op jit(solution)/shard_map/pallas_call | solution.py:259
  488.3 2.2 fusion.73
  490.6 2.7 slice_bitcast_fusion.1
  493.2 10.6 %slice_bitcast_fusion = (f32[1152,1024]{0,1:T(8,128)}, f32[1024,1152]{1,0:T(8,128)}, f32[1024,1152]{1,0:T(8,128)}) fusion(f32[1024,4224]{1,0:T(8,128)} %get-tuple-element.16), kind=kLoop, calls=%fused_computation | loop fusion | bytes 28311552 | tf_op jit(solution)/shard_map/transpose | solution.py:568
  503.8 6.2 %copy.103 = f32[1152,1024]{1,0:T(8,128)} copy(f32[1152,1024]{0,1:T(8,128)} %get-tuple-element.64) | data formatting | bytes 9437184
  510.0 1.3 copy.102
  (172 shorter events, 19.3 us)
Async XLA Ops:
  0.6 114.8 %copy-start = (bf16[1152,1024]{1,0:T(8,128)(2,1)S(1)}, bf16[1152,1024]{1,0:T(8,128)(2,1)}, u32[]{:S(2)}) copy-start(bf16[1152,1024]{1,0:T(8,128)(2,1)} %param.26) | copy-start | bytes 7077892
  0.7 25.5 %copy-start.31 = (bf16[32,1024]{1,0:T(8,128)(2,1)S(1)}, bf16[32,1024]{1,0:T(8,128)(2,1)}, u32[]{:S(2)}) copy-start(bf16[32,1024]{1,0:T(8,128)(2,1)} %param.27) | copy-start | bytes 196612
  5.2 4.0 copy-start.48
  8.1 69.6 %copy-start.39 = (f32[128,32]{0,1:T(8,128)}, f32[128,32]{0,1:T(8,128)S(1)}, u32[]{:S(2)}) copy-start(f32[128,32]{0,1:T(8,128)S(1)} %get-tuple-element.99) | copy-start | bytes 49156
  9.2 78.0 %copy-start.10 = (pred[64,2048]{1,0:T(8,128)(4,1)}, pred[64,2048]{1,0:T(8,128)(4,1)S(1)}, u32[]{:S(2)}) copy-start(pred[64,2048]{1,0:T(8,128)(4,1)S(1)} %broadcast_compare_fusion) | copy-start | bytes 393220
  17.3 60.4 %copy-start.4 = (bf16[128,1024]{1,0:T(8,128)(2,1)}, bf16[128,1024]{1,0:T(8,128)(2,1)S(1)}, u32[]{:S(2)}) copy-start(bf16[128,1024]{1,0:T(8,128)(2,1)S(1)} %all_gather.12) | copy-start | bytes 786436
  19.8 1.6 copy-start.26
  19.9 0.8 copy-start.45
  22.7 55.0 %copy-start.17 = (f32[128,256]{1,0:T(8,128)}, f32[128,256]{1,0:T(8,128)S(1)}, u32[]{:S(2)}) copy-start(f32[128,256]{1,0:T(8,128)S(1)} %fusion.78) | copy-start | bytes 393220
  22.8 56.6 %copy-start.12 = (f32[128,256]{0,1:T(8,128)}, f32[128,256]{0,1:T(8,128)S(1)}, u32[]{:S(2)}) copy-start(f32[128,256]{0,1:T(8,128)S(1)} %copy.78) | copy-start | bytes 393220
  83.2 4.0 copy-start.28
  85.2 4.0 copy-start.2
  92.0 2.0 copy-start.34
  92.0 23.4 %copy-start.23 = (bf16[128,1024]{1,0:T(8,128)(2,1)S(1)}, bf16[128,1024]{1,0:T(8,128)(2,1)}, u32[]{:S(2)}) copy-start(bf16[128,1024]{1,0:T(8,128)(2,1)} %all_gather.14) | copy-start | bytes 786436
  103.2 11.7 %copy-start.6 = (bf16[1024,1152]{1,0:T(8,128)(2,1)S(1)}, bf16[1024,1152]{1,0:T(8,128)(2,1)}, u32[]{:S(2)}) copy-start(bf16[1024,1152]{1,0:T(8,128)(2,1)} %param.24) | copy-start | bytes 7077892
  104.4 40.5 %copy-start.47 = (f32[32]{0:T(128)}, f32[32]{0:T(128)S(1)}, u32[]{:S(2)}) copy-start(f32[32]{0:T(128)S(1)} %add_rsqrt_fusion.2) | copy-start | bytes 388
  112.6 2.3 copy-start.7
  117.2 0.7 copy-start.18
  119.2 24.2 %copy-start.44 = (f32[1024]{0:T(1024)S(1)}, f32[1024]{0:T(1024)}, u32[]{:S(2)}) copy-start(f32[1024]{0:T(1024)} %param.23) | copy-start | bytes 12292
  119.2 25.8 %copy-start.32 = (bf16[32,1024]{1,0:T(8,128)(2,1)S(1)}, bf16[32,1024]{1,0:T(8,128)(2,1)}, u32[]{:S(2)}) copy-start(bf16[32,1024]{1,0:T(8,128)(2,1)} %param.27) | copy-start | bytes 196612
  119.2 34.2 %copy-start.13 = (bf16[256,1024]{1,0:T(8,128)(2,1)S(1)}, bf16[256,1024]{1,0:T(8,128)(2,1)}, u32[]{:S(2)}) copy-start(bf16[256,1024]{1,0:T(8,128)(2,1)} %param.22) | copy-start | bytes 1572868
  128.3 25.7 %copy-start.43 = (f32[2,64,2,2,64]{1,4,3,2,0:T(8,128)S(1)}, f32[2,64,2,2,64]{1,4,3,2,0:T(8,128)}, u32[]{:S(2)}) copy-start(f32[2,64,2,2,64]{1,4,3,2,0:T(8,128)} %get-tuple-element.105) | copy-start | bytes 393220
  144.9 8.5 %copy-start.50 = (f32[32]{0:T(128)}, f32[32]{0:T(128)S(1)}, u32[]{:S(2)}) copy-start(f32[32]{0:T(128)S(1)} %broadcast_multiply_fusion.3) | copy-start | bytes 388
  154.0 0.7 copy-start.37
  154.7 4.5 copy-start.3
  154.7 4.5 copy-start.11
  154.7 4.5 copy-start.38
  154.7 4.5 copy-start.49
  159.2 3.3 copy-start.21
  159.2 3.2 copy-start.22
  166.4 0.6 copy-start.41
  180.2 48.1 %copy-start.40 = (f32[128,32]{0,1:T(8,128)S(1)}, f32[128,32]{0,1:T(8,128)}, u32[]{:S(2)}) copy-start(f32[128,32]{0,1:T(8,128)} %copy-done.39) | copy-start | bytes 49156
  180.2 48.1 %copy-start.27 = (f32[128,128]{0,1:T(8,128)S(1)}, f32[128,128]{0,1:T(8,128)}, u32[]{:S(2)}) copy-start(f32[128,128]{0,1:T(8,128)} %copy-done.26) | copy-start | bytes 196612
  180.2 48.1 %copy-start.51 = (f32[64]{0:T(128)S(1)}, f32[64]{0:T(128)}, u32[]{:S(2)}) copy-start(f32[64]{0:T(128)} %param.21) | copy-start | bytes 772
  180.2 48.2 %copy-start.46 = (f32[128,2]{0,1:T(2,128)S(1)}, f32[128,2]{0,1:T(2,128)}, u32[]{:S(2)}) copy-start(f32[128,2]{0,1:T(2,128)} %copy-done.45) | copy-start | bytes 3076
  180.2 48.2 %copy-start.52 = (f32[128]{0:T(128)S(1)}, f32[128]{0:T(128)}, u32[]{:S(2)}) copy-start(f32[128]{0:T(128)} %mul.551) | copy-start | bytes 1540
  180.2 48.4 %copy-start.14 = (f32[128,1024]{1,0:T(8,128)S(1)}, f32[128,1024]{1,0:T(8,128)}, u32[]{:S(2)}) copy-start(f32[128,1024]{1,0:T(8,128)} %fusion.82) | copy-start | bytes 1572868
  180.2 48.4 %copy-start.29 = (bf16[1024,128]{1,0:T(8,128)(2,1)S(1)}, bf16[1024,128]{1,0:T(8,128)(2,1)}, u32[]{:S(2)}) copy-start(bf16[1024,128]{1,0:T(8,128)(2,1)} %param.18) | copy-start | bytes 786436
  180.3 48.6 %copy-start.25 = (bf16[1024,128]{1,0:T(8,128)(2,1)S(1)}, bf16[1024,128]{1,0:T(8,128)(2,1)}, u32[]{:S(2)}) copy-start(bf16[1024,128]{1,0:T(8,128)(2,1)} %param.19) | copy-start | bytes 786436
  185.8 54.8 %copy-start.15 = (bf16[32,1024]{1,0:T(8,128)(2,1)S(1)}, bf16[32,1024]{1,0:T(8,128)(2,1)}, u32[]{:S(2)}) copy-start(bf16[32,1024]{1,0:T(8,128)(2,1)} %param.14) | copy-start | bytes 196612
  185.8 55.9 %copy-start.9 = (f32[32,1024]{1,0:T(8,128)S(1)}, f32[32,1024]{1,0:T(8,128)}, u32[]{:S(2)}) copy-start(f32[32,1024]{1,0:T(8,128)} %shard_map.240) | copy-start | bytes 393220
  185.8 55.9 %copy-start.33 = (bf16[32,1024]{1,0:T(8,128)(2,1)S(1)}, bf16[32,1024]{1,0:T(8,128)(2,1)}, u32[]{:S(2)}) copy-start(bf16[32,1024]{1,0:T(8,128)(2,1)} %param.27) | copy-start | bytes 196612
  185.8 55.9 %copy-start.36 = (f32[32,1024]{1,0:T(8,128)S(1)}, f32[32,1024]{1,0:T(8,128)}, u32[]{:S(2)}) copy-start(f32[32,1024]{1,0:T(8,128)} %shard_map.239) | copy-start | bytes 393220
  185.8 67.2 %copy-start.5 = (bf16[128,1024]{1,0:T(8,128)(2,1)S(1)}, bf16[128,1024]{1,0:T(8,128)(2,1)}, u32[]{:S(2)}) copy-start(bf16[128,1024]{1,0:T(8,128)(2,1)} %copy-done.4) | copy-start | bytes 786436
  185.8 67.2 %copy-start.42 = (bf16[128,256]{1,0:T(8,128)(2,1)S(1)}, bf16[128,256]{1,0:T(8,128)(2,1)}, u32[]{:S(2)}) copy-start(bf16[128,256]{1,0:T(8,128)(2,1)} %copy-done.41) | copy-start | bytes 196612
  185.8 70.4 %copy-start.35 = (bf16[128,256]{1,0:T(8,128)(2,1)S(1)}, bf16[128,256]{1,0:T(8,128)(2,1)}, u32[]{:S(2)}) copy-start(bf16[128,256]{1,0:T(8,128)(2,1)} %copy-done.34) | copy-start | bytes 196612
  227.3 28.0 %copy-start.30 = (f32[128,256]{1,0:T(8,128)S(1)}, f32[128,256]{1,0:T(8,128)}, u32[]{:S(2)}) copy-start(f32[128,256]{1,0:T(8,128)} %shard_map.241) | copy-start | bytes 393220
  227.3 30.1 %copy-start.8 = (bf16[128,1024]{1,0:T(8,128)(2,1)S(1)}, bf16[128,1024]{1,0:T(8,128)(2,1)}, u32[]{:S(2)}) copy-start(bf16[128,1024]{1,0:T(8,128)(2,1)} %copy-done.7) | copy-start | bytes 786436
  227.3 30.1 %copy-start.16 = (bf16[128,1152]{1,0:T(8,128)(2,1)S(1)}, bf16[128,1152]{1,0:T(8,128)(2,1)}, u32[]{:S(2)}) copy-start(bf16[128,1152]{1,0:T(8,128)(2,1)} %get-tuple-element.74) | copy-start | bytes 884740
  228.9 30.8 %copy-start.20 = (bf16[128,1152]{1,0:T(8,128)(2,1)S(1)}, bf16[128,1152]{1,0:T(8,128)(2,1)}, u32[]{:S(2)}) copy-start(bf16[128,1152]{1,0:T(8,128)(2,1)} %get-tuple-element.73) | copy-start | bytes 884740
  253.1 8.9 %copy-start.19 = (bf16[128,1152]{1,0:T(8,128)(2,1)S(1)}, bf16[128,1152]{1,0:T(8,128)(2,1)}, u32[]{:S(2)}) copy-start(bf16[128,1152]{1,0:T(8,128)(2,1)} %copy-done.18) | copy-start | bytes 884740
  253.1 8.9 %copy-start.24 = (bf16[128,1024]{1,0:T(8,128)(2,1)S(1)}, bf16[128,1024]{1,0:T(8,128)(2,1)}, u32[]{:S(2)}) copy-start(bf16[128,1024]{1,0:T(8,128)(2,1)} %all_gather.14) | copy-start | bytes 786436
  503.8 7.5 %copy-start.1 = (bf16[1152,1024]{1,0:T(8,128)(2,1)S(1)}, bf16[1152,1024]{1,0:T(8,128)(2,1)}, u32[]{:S(2)}) copy-start(bf16[1152,1024]{1,0:T(8,128)(2,1)} %param.26) | copy-start | bytes 7077892
